TPU v7x, 768 devices: a whole 4x8x12 slice. The times are simulated.
768 devices in a mesh: cluster: 24 (over z, core), member: 32 (over x, y).
Axes of the slice: x: 4, y: 8, z: 12, core: 2. Of those that a mesh axis runs over, the one named last changes fastest.
Arguments:
- dual_load: float32 [24, 32, 64, 2, 1024], P('cluster', 'member'), may hold values from -110 to 110
- dual_operator: bfloat16 [2048, 2048], replicated, may hold values from -1.5859375 to 3.5859375, as said below
- index_map: int32 [24, 32, 2048], P('cluster', 'member'), may hold values from 0 to 2047, as said below
- stiffness: float32 [24, 32], P('cluster', 'member'), may hold values from 1 to 10
- coarse_basis: float32 [24, 32, 6, 2048], P('cluster', 'member'), may hold values from -2.5 to 2.5
- dirichlet_blocks: bfloat16 [24, 32, 16, 128, 128], P('cluster', 'member'), may hold values from -1 to 2.5, as said below
- coarse_inverse: float32 [144, 144], replicated, may hold values from -1 to 1, as said below
Outputs:
- multipliers: float32 [24, 32, 64, 2, 1024], P('cluster', 'member')
- residual: float32 [24, 32, 64, 2, 1024], P('cluster', 'member')
Inputs may be any that keep to these rules, and one draw needn't show every extreme that they name: `dual_operator`: symmetric. `dirichlet_blocks`: each block is symmetric. `coarse_inverse`: symmetric. `index_map`: each subdomain's row names every position once.
All inputs are finite; a program needn't handle non-finite values.
Results may differ from a plain program's by a relative error of at most 0.0038.
Values sent between devices are 32-bit elements; how exact they have to be, the bound alone decides.
A program may use at most 64 MiB of HBM per device.

v0:
```python
import jax
import jax.numpy as jnp
from jax import lax
from jax.sharding import PartitionSpec as P

ITERS = 2


exact_precision = lax.Precision.HIGHEST


def with_halo(array, sides, width):
    for axis, dim in sides:
        count, length = (lax.axis_size(axis), array.shape[dim])
        up = [(i, (i + 1) % count) for i in range(count - 1)]
        down = [(j, i) for i, j in up]
        last = lax.slice_in_dim(array, length - width, length, axis=dim)
        initial = lax.slice_in_dim(array, 0, width, axis=dim)
        before = lax.ppermute(last, axis, up)
        after = lax.ppermute(initial, axis, down)
        array = jnp.concatenate([before, array, after], axis=dim)
    return array


def per_device(
    dual_load, dual_operator, index_map, stiffness, coarse_basis, dirichlet_blocks, coarse_inverse
):
    load_cases = dual_load.shape[2]
    face_slots = dual_load.shape[4]
    slot_count = 2 * face_slots
    ordering = index_map.reshape(slot_count)
    inverse = (
        jnp.zeros((slot_count,), jnp.int32)
        .at[ordering]
        .set(jnp.arange(slot_count, dtype=jnp.int32))
    )
    softness = 1.0 / stiffness.reshape(())
    basis_rows = coarse_basis.reshape(coarse_basis.shape[2], slot_count)
    mode_count = basis_rows.shape[0]
    blocks = dirichlet_blocks.reshape(dirichlet_blocks.shape[2:])
    block_count = blocks.shape[0]
    block_size = blocks.shape[1]
    cluster_id = lax.axis_index("cluster")
    member_id = lax.axis_index("member")
    cluster_total = lax.axis_size("cluster")
    member_total = lax.axis_size("member")
    chain_pos = cluster_id * member_total + member_id
    chain_len = cluster_total * member_total
    low_side = jnp.where(chain_pos > 0, 0.5, 1.0)
    high_side = jnp.where(chain_pos < chain_len - 1, 0.5, 1.0)
    weights = jnp.stack([low_side, high_side]).astype(jnp.float32).reshape(1, 2, 1)

    def assemble(vector):
        padded = with_halo(vector, ((("cluster", "member"), 1),), 1)
        return vector + jnp.stack([padded[:, 0], padded[:, 3]], axis=1)

    def restrict(vector):
        return lax.dot_general(
            vector.reshape(load_cases, slot_count),
            basis_rows,
            (((1,), (1,)), ((), ())),
            precision=exact_precision,
        )

    def expand(own_amounts):
        return jnp.dot(own_amounts, basis_rows, precision=exact_precision).reshape(
            load_cases, 2, face_slots
        )

    residual = assemble(dual_load.reshape(load_cases, 2, face_slots))
    multipliers = jnp.zeros_like(residual)
    direction = residual
    rho_prev = None
    own_rows = lax.dynamic_slice_in_dim(coarse_inverse, cluster_id * mode_count, mode_count, 0)

    def add_cluster(segment):
        return lax.dot_general(
            segment, own_rows, (((1,), (1,)), ((), ())), precision=exact_precision
        )

    def project(vector):
        summed = lax.psum(restrict(vector), "member")
        own_amounts = add_cluster(lax.all_gather(summed, "cluster", axis=1, tiled=True))
        return vector - assemble(expand(own_amounts))

    def inner(left, right):
        return lax.psum(jnp.sum(weights * left * right, axis=(1, 2)), ("cluster", "member"))

    for sweep in range(ITERS):
        projected = project(residual)
        scaled = (
            (weights * projected).astype(jnp.bfloat16).reshape(load_cases, block_count, block_size)
        )
        blocked = jnp.einsum("rnj,nij->rni", scaled, blocks, preferred_element_type=jnp.float32)
        search = project(assemble(weights * blocked.reshape(load_cases, 2, face_slots)))
        rho_now = inner(projected, search)
        if sweep == 0:
            direction = search
        else:
            direction = search + (rho_now / rho_prev)[:, None, None] * direction
        rho_prev = rho_now
        flattened = direction.astype(jnp.bfloat16).reshape(load_cases, slot_count)
        local_order = jnp.take(flattened, inverse, axis=1)
        product = jnp.dot(local_order, dual_operator, preferred_element_type=jnp.float32)
        applied = assemble(
            (softness * jnp.take(product, ordering, axis=1)).reshape(load_cases, 2, face_slots)
        )
        step_size = (rho_now / inner(direction, applied))[:, None, None]
        multipliers = multipliers + step_size * direction
        residual = residual - step_size * applied
    return (multipliers.reshape(dual_load.shape), residual.reshape(dual_load.shape))


def solution(mesh):
    in_specs = (
        P("cluster", "member", None, None, None),
        P(),
        P("cluster", "member", None),
        P("cluster", "member"),
        P("cluster", "member", None, None),
        P("cluster", "member", None, None, None),
        P(),
    )
    out_specs = (P("cluster", "member", None, None, None), P("cluster", "member", None, None, None))
    return jax.shard_map(
        per_device, mesh=mesh, in_specs=in_specs, out_specs=out_specs, check_vma=False
    )
```

profile of v0, /device:TPU:1, one launch (start us, length us, event | category | flops | bytes accessed | tf_op | source)
XLA Modules:
  0.0 944.2 jit_solution(2211536766368016745)
XLA Ops:
  2.0 4.0 collective-permute-start
  6.0 6.6 collective-permute-start.1
  19.2 63.7 %psum.56 = f32[64,6]{0,1:T(8,128)S(1)} all-reduce(f32[64,6]{0,1:T(8,128)S(1)} %fusion.39), channel_id=1, replica_groups=mesh['cluster'=24,'member'=32] {'member'}, use_global_device_ids=true, to_apply=%region_0.0 | all-reduce | flops 384 | bytes 3072 | tf_op jit(solution)/shard_map/psum | solution.py:82
  82.9 46.0 %all-gather = f32[24,6,64]{2,1,0:T(8,128)S(1)} all-gather(f32[1,6,64]{2,1,0:T(8,128)S(1)} %bitcast.166), channel_id=1, replica_groups=mesh['cluster'=24,'member'=32] {'cluster'}, dimensions={0}, use_global_device_ids=true | all-gather | bytes 38400 | tf_op jit(solution)/shard_map/all_gather | solution.py:83
  132.4 7.0 collective-permute-start.3
  141.5 4.0 collective-permute-done.3
  150.9 7.7 collective-permute-start.5
  158.7 8.0 scatter_custom_fusion
  168.2 56.6 %psum.57 = f32[64,6]{0,1:T(8,128)S(1)} all-reduce(f32[64,6]{0,1:T(8,128)S(1)} %fusion.35), channel_id=1, replica_groups=mesh['cluster'=24,'member'=32] {'member'}, use_global_device_ids=true, to_apply=%region_1.2 | all-reduce | flops 384 | bytes 3072 | tf_op jit(solution)/shard_map/psum | solution.py:82
  224.7 37.5 %all-gather.1 = f32[24,6,64]{2,1,0:T(8,128)S(1)} all-gather(f32[1,6,64]{2,1,0:T(8,128)S(1)} %bitcast.167), channel_id=1, replica_groups=mesh['cluster'=24,'member'=32] {'cluster'}, dimensions={0}, use_global_device_ids=true | all-gather | bytes 38400 | tf_op jit(solution)/shard_map/all_gather | solution.py:83
  265.7 7.1 collective-permute-start.7
  274.8 4.0 collective-permute-done.7
  280.4 8.1 gather_fusion
  288.5 7.2 fusion.14
  295.7 7.6 gather_fusion.1
  306.9 7.7 collective-permute-start.9
  323.6 107.8 %all-reduce = (f32[64]{0:T(128)S(1)}, f32[64]{0:T(128)S(1)}) all-reduce(f32[64]{0:T(128)S(1)} %get-tuple-element.13, f32[64]{0:T(128)S(1)} %get-tuple-element.12), channel_id=1, replica_groups=mesh['cluster'=24,'member'=32] {'cluster','member'}, use_global_device_ids=true, to_apply=%region_3.4 | all-reduce | flops 128 | bytes 1024 | tf_op jit(solution)/shard_map/psum | solution.py:87
  433.4 55.7 %psum.60 = f32[64,6]{0,1:T(8,128)S(1)} all-reduce(f32[64,6]{0,1:T(8,128)S(1)} %fusion.20), channel_id=1, replica_groups=mesh['cluster'=24,'member'=32] {'member'}, use_global_device_ids=true, to_apply=%region_7.10 | all-reduce | flops 384 | bytes 3072 | tf_op jit(solution)/shard_map/psum | solution.py:82
  489.1 35.2 %all-gather.2 = f32[24,6,64]{2,1,0:T(8,128)S(1)} all-gather(f32[1,6,64]{2,1,0:T(8,128)S(1)} %bitcast.168), channel_id=1, replica_groups=mesh['cluster'=24,'member'=32] {'cluster'}, dimensions={0}, use_global_device_ids=true | all-gather | bytes 38400 | tf_op jit(solution)/shard_map/all_gather | solution.py:83
  529.6 5.2 collective-permute-start.11
  544.1 9.5 %collective-permute-start.13 = (f32[64,1,1024]{2,0,1:T(8,128)S(1)}, f32[64,1,1024]{2,0,1:T(8,128)S(1)}, u32[]{:S(2)}, u32[]{:S(2)}) collective-permute-start(f32[64,1,1024]{2,0,1:T(8,128)S(1)} %get-tuple-element.29), channel_id=1, source_target_pairs={{1,0},{2,1},{3,2},{4,3},{5,4},{6,5},{7,6},{8,7},{9,8},{10,9},{11,1... | collective-permute-start | bytes 786440 | tf_op jit(solution)/shard_map/ppermute | solution.py:20
  555.7 4.0 collective-permute-done.13
  561.2 59.2 %psum.61 = f32[64,6]{0,1:T(8,128)S(1)} all-reduce(f32[64,6]{0,1:T(8,128)S(1)} %fusion.37), channel_id=1, replica_groups=mesh['cluster'=24,'member'=32] {'member'}, use_global_device_ids=true, to_apply=%region_8.11 | all-reduce | flops 384 | bytes 3072 | tf_op jit(solution)/shard_map/psum | solution.py:82
  620.3 37.2 %all-gather.3 = f32[24,6,64]{2,1,0:T(8,128)S(1)} all-gather(f32[1,6,64]{2,1,0:T(8,128)S(1)} %bitcast.169), channel_id=1, replica_groups=mesh['cluster'=24,'member'=32] {'cluster'}, dimensions={0}, use_global_device_ids=true | all-gather | bytes 38400 | tf_op jit(solution)/shard_map/all_gather | solution.py:83
  661.1 7.2 collective-permute-start.15
  672.9 111.8 %psum.62 = f32[64]{0:T(128)S(1)} all-reduce(f32[64]{0:T(128)S(1)} %get-tuple-element.16), channel_id=1, replica_groups=mesh['cluster'=24,'member'=32] {'cluster','member'}, use_global_device_ids=true, to_apply=%region_10.13 | all-reduce | flops 64 | bytes 512 | tf_op jit(solution)/shard_map/psum | solution.py:87
  785.9 8.1 gather_fusion.2
  793.9 7.2 fusion.12
  801.1 7.6 gather_fusion.3
  815.1 7.0 collective-permute-start.17
  824.5 4.0 collective-permute-done.17
  829.9 109.6 %psum.63 = f32[64]{0:T(128)S(1)} all-reduce(f32[64]{0:T(128)S(1)} %fusion.7), channel_id=1, replica_groups=mesh['cluster'=24,'member'=32] {'cluster','member'}, use_global_device_ids=true, to_apply=%region_12.15 | all-reduce | flops 64 | bytes 512 | tf_op jit(solution)/shard_map/psum | solution.py:87
  (141 shorter events, 83.2 us)
Async XLA Ops:
  0.6 146.4 %copy-start = (bf16[1,1,16,128,128]{4,3,2,1,0:T(8,128)(2,1)S(1)}, bf16[1,1,16,128,128]{4,3,2,1,0:T(8,128)(2,1)}, u32[]{:S(2)}) copy-start(bf16[1,1,16,128,128]{4,3,2,1,0:T(8,128)(2,1)} %param.16) | copy-start | bytes 1572868
  0.6 144.8 %copy-start.1 = (f32[1,1,64,2,1024]{4,3,2,1,0:T(2,128)S(1)}, f32[1,1,64,2,1024]{4,3,2,1,0:T(2,128)}, u32[]{:S(2)}) copy-start(f32[1,1,64,2,1024]{4,3,2,1,0:T(2,128)} %param.11) | copy-start | bytes 1572868
  2.0 12.7 %collective-permute-start = (f32[64,1,1024]{2,0,1:T(8,128)S(1)}, f32[64,1,1024]{2,0,1:T(8,128)S(1)}, u32[]{:S(2)}, u32[]{:S(2)}) collective-permute-start(f32[64,1,1024]{2,0,1:T(8,128)S(1)} %get-tuple-element.41), channel_id=1, source_target_pairs={{0,1},{1,2},{2,3},{3,4},{4,5},{5,6},{6,7},{7,8},{8,9},{9,10},{10,1... | collective-permute-start | bytes 786440 | tf_op jit(solution)/shard_map/ppermute | solution.py:19
  6.0 9.9 %collective-permute-start.1 = (f32[64,1,1024]{2,0,1:T(8,128)S(1)}, f32[64,1,1024]{2,0,1:T(8,128)S(1)}, u32[]{:S(2)}, u32[]{:S(2)}) collective-permute-start(f32[64,1,1024]{2,0,1:T(8,128)S(1)} %get-tuple-element.40), channel_id=1, source_target_pairs={{1,0},{2,1},{3,2},{4,3},{5,4},{6,5},{7,6},{8,7},{9,8},{10,9},{11,1... | collective-permute-start | bytes 786440 | tf_op jit(solution)/shard_map/ppermute | solution.py:20
  13.4 145.2 %copy-start.12 = (s32[1,1,2048]{2,1,0:T(1,128)S(1)}, s32[1,1,2048]{2,1,0:T(1,128)}, u32[]{:S(2)}) copy-start(s32[1,1,2048]{2,1,0:T(1,128)} %param.13) | copy-start | bytes 24580
  14.7 115.1 %copy-start.8 = (f32[64,1,1024]{2,0,1:T(8,128)}, f32[64,1,1024]{2,0,1:T(8,128)S(1)}, u32[]{:S(2)}) copy-start(f32[64,1,1024]{2,0,1:T(8,128)S(1)} %collective-permute-done) | copy-start | bytes 786436
  15.9 113.9 %copy-start.9 = (f32[64,1,1024]{2,0,1:T(8,128)}, f32[64,1,1024]{2,0,1:T(8,128)S(1)}, u32[]{:S(2)}) copy-start(f32[64,1,1024]{2,0,1:T(8,128)S(1)} %collective-permute-done.1) | copy-start | bytes 786436
  17.3 150.4 %copy-start.4 = (f32[1,1,6,2048]{3,1,2,0:T(1,128)S(1)}, f32[1,1,6,2048]{3,1,2,0:T(1,128)}, u32[]{:S(2)}) copy-start(f32[1,1,6,2048]{3,1,2,0:T(1,128)} %param.15) | copy-start | bytes 147460
  130.5 11.0 %collective-permute-start.2 = (f32[64,1,1024]{2,0,1:T(8,128)S(1)}, f32[64,1,1024]{2,0,1:T(8,128)S(1)}, u32[]{:S(2)}, u32[]{:S(2)}) collective-permute-start(f32[64,1,1024]{2,0,1:T(8,128)S(1)} %get-tuple-element.38), channel_id=1, source_target_pairs={{0,1},{1,2},{2,3},{3,4},{4,5},{5,6},{6,7},{7,8},{8,9},{9,10},{10,1... | collective-permute-start | bytes 786440 | tf_op jit(solution)/shard_map/ppermute | solution.py:19
  132.4 13.1 %collective-permute-start.3 = (f32[64,1,1024]{2,0,1:T(8,128)S(1)}, f32[64,1,1024]{2,0,1:T(8,128)S(1)}, u32[]{:S(2)}, u32[]{:S(2)}) collective-permute-start(f32[64,1,1024]{2,0,1:T(8,128)S(1)} %get-tuple-element.39), channel_id=1, source_target_pairs={{1,0},{2,1},{3,2},{4,3},{5,4},{6,5},{7,6},{8,7},{9,8},{10,9},{11,1... | collective-permute-start | bytes 786440 | tf_op jit(solution)/shard_map/ppermute | solution.py:20
  139.5 134.6 %copy-start.13 = (f32[2]{0:T(128)}, f32[2]{0:T(128)S(1)}, u32[]{:S(2)}) copy-start(f32[2]{0:T(128)S(1)} %pad_maximum_fusion) | copy-start | bytes 28
  149.0 18.3 %collective-permute-start.4 = (f32[64,1,1024]{2,0,1:T(8,128)}, f32[64,1,1024]{2,0,1:T(8,128)S(1)}, u32[]{:S(2)}, u32[]{:S(2)}) collective-permute-start(f32[64,1,1024]{2,0,1:T(8,128)} %get-tuple-element.36), channel_id=1, source_target_pairs={{0,1},{1,2},{2,3},{3,4},{4,5},{5,6},{6,7},{7,8},{8,9},{9,10},{10,1... | collective-permute-start | bytes 786440 | tf_op jit(solution)/shard_map/ppermute | solution.py:19
  150.9 16.4 %collective-permute-start.5 = (f32[64,1,1024]{2,0,1:T(8,128)S(1)}, f32[64,1,1024]{2,0,1:T(8,128)S(1)}, u32[]{:S(2)}, u32[]{:S(2)}) collective-permute-start(f32[64,1,1024]{2,0,1:T(8,128)S(1)} %get-tuple-element.37), channel_id=1, source_target_pairs={{1,0},{2,1},{3,2},{4,3},{5,4},{6,5},{7,6},{8,7},{9,8},{10,9},{11,1... | collective-permute-start | bytes 786440 | tf_op jit(solution)/shard_map/ppermute | solution.py:20
  167.3 107.5 %copy-start.5 = (f32[64,1,1024]{2,0,1:T(8,128)}, f32[64,1,1024]{2,0,1:T(8,128)S(1)}, u32[]{:S(2)}) copy-start(f32[64,1,1024]{2,0,1:T(8,128)S(1)} %collective-permute-done.4) | copy-start | bytes 786436
  167.4 107.5 %copy-start.6 = (f32[64,1,1024]{2,0,1:T(8,128)}, f32[64,1,1024]{2,0,1:T(8,128)S(1)}, u32[]{:S(2)}) copy-start(f32[64,1,1024]{2,0,1:T(8,128)S(1)} %collective-permute-done.5) | copy-start | bytes 786436
  263.8 11.0 %collective-permute-start.6 = (f32[64,1,1024]{2,0,1:T(8,128)S(1)}, f32[64,1,1024]{2,0,1:T(8,128)S(1)}, u32[]{:S(2)}, u32[]{:S(2)}) collective-permute-start(f32[64,1,1024]{2,0,1:T(8,128)S(1)} %get-tuple-element.34), channel_id=1, source_target_pairs={{0,1},{1,2},{2,3},{3,4},{4,5},{5,6},{6,7},{7,8},{8,9},{9,10},{10,1... | collective-permute-start | bytes 786440 | tf_op jit(solution)/shard_map/ppermute | solution.py:19
  265.7 13.1 %collective-permute-start.7 = (f32[64,1,1024]{2,0,1:T(8,128)S(1)}, f32[64,1,1024]{2,0,1:T(8,128)S(1)}, u32[]{:S(2)}, u32[]{:S(2)}) collective-permute-start(f32[64,1,1024]{2,0,1:T(8,128)S(1)} %get-tuple-element.35), channel_id=1, source_target_pairs={{1,0},{2,1},{3,2},{4,3},{5,4},{6,5},{7,6},{8,7},{9,8},{10,9},{11,1... | collective-permute-start | bytes 786440 | tf_op jit(solution)/shard_map/ppermute | solution.py:20
  295.7 26.6 %copy-start.14 = (f32[2]{0:T(128)S(1)}, f32[2]{0:T(128)}, u32[]{:S(2)}) copy-start(f32[2]{0:T(128)} %copy-done.13) | copy-start | bytes 28
  305.0 11.8 %collective-permute-start.8 = (f32[64,1,1024]{2,0,1:T(8,128)S(1)}, f32[64,1,1024]{2,0,1:T(8,128)S(1)}, u32[]{:S(2)}, u32[]{:S(2)}) collective-permute-start(f32[64,1,1024]{2,0,1:T(8,128)S(1)} %get-tuple-element.33), channel_id=1, source_target_pairs={{0,1},{1,2},{2,3},{3,4},{4,5},{5,6},{6,7},{7,8},{8,9},{9,10},{10,1... | collective-permute-start | bytes 786440 | tf_op jit(solution)/shard_map/ppermute | solution.py:19
  306.9 13.8 %collective-permute-start.9 = (f32[64,1,1024]{2,0,1:T(8,128)S(1)}, f32[64,1,1024]{2,0,1:T(8,128)S(1)}, u32[]{:S(2)}, u32[]{:S(2)}) collective-permute-start(f32[64,1,1024]{2,0,1:T(8,128)S(1)} %get-tuple-element.32), channel_id=1, source_target_pairs={{1,0},{2,1},{3,2},{4,3},{5,4},{6,5},{7,6},{8,7},{9,8},{10,9},{11,1... | collective-permute-start | bytes 786440 | tf_op jit(solution)/shard_map/ppermute | solution.py:20
  431.4 109.2 %copy-start.17 = (f32[64]{0:T(128)}, f32[64]{0:T(128)S(1)}, u32[]{:S(2)}) copy-start(f32[64]{0:T(128)S(1)} %get-tuple-element.14) | copy-start | bytes 772
  525.9 11.0 %collective-permute-start.10 = (f32[64,1,1024]{2,0,1:T(8,128)S(1)}, f32[64,1,1024]{2,0,1:T(8,128)S(1)}, u32[]{:S(2)}, u32[]{:S(2)}) collective-permute-start(f32[64,1,1024]{2,0,1:T(8,128)S(1)} %get-tuple-element.30), channel_id=1, source_target_pairs={{0,1},{1,2},{2,3},{3,4},{4,5},{5,6},{6,7},{7,8},{8,9},{9,10},{10,1... | collective-permute-start | bytes 786440 | tf_op jit(solution)/shard_map/ppermute | solution.py:19
  529.6 9.3 collective-permute-start.11
  541.0 252.9 %copy-start.16 = (pred[2048]{0:T(1024)(128)(4,1)S(1)}, pred[2048]{0:T(1024)(128)(4,1)}, u32[]{:S(2)}) copy-start(pred[2048]{0:T(1024)(128)(4,1)} %compare_and_fusion.1) | copy-start | bytes 6148
  541.9 13.8 %collective-permute-start.12 = (f32[64,1,1024]{2,0,1:T(8,128)S(1)}, f32[64,1,1024]{2,0,1:T(8,128)S(1)}, u32[]{:S(2)}, u32[]{:S(2)}) collective-permute-start(f32[64,1,1024]{2,0,1:T(8,128)S(1)} %get-tuple-element.28), channel_id=1, source_target_pairs={{0,1},{1,2},{2,3},{3,4},{4,5},{5,6},{6,7},{7,8},{8,9},{9,10},{10,1... | collective-permute-start | bytes 786440 | tf_op jit(solution)/shard_map/ppermute | solution.py:19
  544.1 15.6 %collective-permute-start.13 = (f32[64,1,1024]{2,0,1:T(8,128)S(1)}, f32[64,1,1024]{2,0,1:T(8,128)S(1)}, u32[]{:S(2)}, u32[]{:S(2)}) collective-permute-start(f32[64,1,1024]{2,0,1:T(8,128)S(1)} %get-tuple-element.29), channel_id=1, source_target_pairs={{1,0},{2,1},{3,2},{4,3},{5,4},{6,5},{7,6},{8,7},{9,8},{10,9},{11,1... | collective-permute-start | bytes 786440 | tf_op jit(solution)/shard_map/ppermute | solution.py:20
  659.2 11.0 %collective-permute-start.14 = (f32[64,1,1024]{2,0,1:T(8,128)S(1)}, f32[64,1,1024]{2,0,1:T(8,128)S(1)}, u32[]{:S(2)}, u32[]{:S(2)}) collective-permute-start(f32[64,1,1024]{2,0,1:T(8,128)S(1)} %get-tuple-element.26), channel_id=1, source_target_pairs={{0,1},{1,2},{2,3},{3,4},{4,5},{5,6},{6,7},{7,8},{8,9},{9,10},{10,1... | collective-permute-start | bytes 786440 | tf_op jit(solution)/shard_map/ppermute | solution.py:19
  661.1 10.3 %collective-permute-start.15 = (f32[64,1,1024]{2,0,1:T(8,128)S(1)}, f32[64,1,1024]{2,0,1:T(8,128)S(1)}, u32[]{:S(2)}, u32[]{:S(2)}) collective-permute-start(f32[64,1,1024]{2,0,1:T(8,128)S(1)} %get-tuple-element.27), channel_id=1, source_target_pairs={{1,0},{2,1},{3,2},{4,3},{5,4},{6,5},{7,6},{8,7},{9,8},{10,9},{11,1... | collective-permute-start | bytes 786440 | tf_op jit(solution)/shard_map/ppermute | solution.py:20
  672.9 112.9 %copy-start.2 = (f32[64,2,1024]{2,0,1:T(8,128)}, f32[64,2,1024]{2,0,1:T(8,128)S(1)}, u32[]{:S(2)}) copy-start(f32[64,2,1024]{2,0,1:T(8,128)S(1)} %get-tuple-element.17) | copy-start | bytes 1572868
  808.7 130.7 %copy-start.3 = (f32[64,2,1024]{2,0,1:T(8,128)S(1)}, f32[64,2,1024]{2,0,1:T(8,128)}, u32[]{:S(2)}) copy-start(f32[64,2,1024]{2,0,1:T(8,128)} %copy-done.2) | copy-start | bytes 1572868
  813.1 11.4 %collective-permute-start.16 = (f32[64,1,1024]{2,0,1:T(8,128)}, f32[64,1,1024]{2,0,1:T(8,128)S(1)}, u32[]{:S(2)}, u32[]{:S(2)}) collective-permute-start(f32[64,1,1024]{2,0,1:T(8,128)} %get-tuple-element.24), channel_id=1, source_target_pairs={{0,1},{1,2},{2,3},{3,4},{4,5},{5,6},{6,7},{7,8},{8,9},{9,10},{10,1... | collective-permute-start | bytes 786440 | tf_op jit(solution)/shard_map/ppermute | solution.py:19
  815.1 13.4 %collective-permute-start.17 = (f32[64,1,1024]{2,0,1:T(8,128)}, f32[64,1,1024]{2,0,1:T(8,128)}, u32[]{:S(2)}, u32[]{:S(2)}) collective-permute-start(f32[64,1,1024]{2,0,1:T(8,128)} %get-tuple-element.25), channel_id=1, source_target_pairs={{1,0},{2,1},{3,2},{4,3},{5,4},{6,5},{7,6},{8,7},{9,8},{10,9},{11,1... | collective-permute-start | bytes 786440 | tf_op jit(solution)/shard_map/ppermute | solution.py:20
  (4 other events, 21.8 us)
where the time goes:
time: 946 us; the launch traced here: 944 us
  blocking collectives  720 us (76%)
  starting transfers between devices  86.3 us (9%)
  local copies, waits for them, and re-layouts  59.7 us (6%)
  waiting for transfers between devices  34.5 us (4%)
  matrix products  25.8 us (3%)
  other arithmetic  15.6 us (2%)
    psum x3, blocking collectives, inner(): lax.psum(jnp.sum(weights * left * right, axis=(1, 2)), ('cluster', 'membe...  329 us
    psum x4, blocking collectives, project(): summed = lax.psum(restrict(vector), 'member')  235 us
    all_gather x4, blocking collectives, project(): lax.all_gather(summed, 'cluster', axis=1, tiled=True)  156 us
    ppermute x9, starting transfers between devices, with_halo(): after = lax.ppermute(initial, axis, down)  65 us
    ppermute x9, waiting for transfers between devices, with_halo(): after = lax.ppermute(initial, axis, down)  24.2 us
    ppermute x9, starting transfers between devices, with_halo(): before = lax.ppermute(last, axis, up)  21.4 us
    gather x4, local copies, waits for them, and re-layouts, per_device(): jnp.take(product, ordering, axis=1)  19.1 us
  transfers between devices with their start and end apart: 18, of which 15 were waited for; matrix products, arithmetic and copies ran while one was open for 2% of the time, Pallas kernels for 0%

commit v1 on v0

v1 whole, which is shorter than its diff:
```python
import functools
import jax
import jax.numpy as jnp
from jax import lax
from jax.experimental import pallas as pl
from jax.experimental.pallas import tpu as pltpu
from jax.sharding import PartitionSpec as P

MESH = pl.DeviceIdType.MESH
NY = 8
CORES = 2
GROUP = 8
SPAN = 32
LANES = 128
HALOS = 5
SUMS = 5
F32 = jnp.float32
BF16 = jnp.bfloat16


def nt(a, b):
    return lax.dot_general(a, b, (((1,), (1,)), ((), ())), preferred_element_type=F32)


def mm(a, b):
    return jnp.dot(a, b, preferred_element_type=F32)


def exact(a, b):
    return jnp.dot(a, b, precision=lax.Precision.HIGHEST, preferred_element_type=F32)


def split(v):
    high = v.astype(BF16)
    return high, (v - high.astype(F32)).astype(BF16)


def kernel(
    load_ref,
    basis_ref,
    blocks_ref,
    coarse_ref,
    index_ref,
    stiff_ref,
    oper_hbm,
    mult_out,
    resid_out,
    oper,
    own_basis,
    nbr_basis,
    span_f,
    span_h,
    span_l,
    coarse,
    inverse,
    halo,
    sent,
    resid,
    proj,
    search0,
    search1,
    image_q,
    temp,
    ybuf,
    xbuf,
    zbuf,
    oper_sem,
    basis_s,
    basis_r,
    halo_s,
    halo_r,
    y_s,
    y_r,
    x_s,
    x_r,
    z_s,
    z_r,
    c_s,
    c_r,
):
    loads, slots = load_ref.shape
    face = slots // 2
    chunks = slots // LANES
    modes = basis_ref.shape[0]
    nblock, block = blocks_ref.shape[:2]
    nz = zbuf.shape[2] - 2
    nx = xbuf.shape[1]
    ny = ybuf.shape[1]
    members = nx * ny
    c = lax.axis_index("cluster")
    m = lax.axis_index("member")
    z, core = c // CORES, lax.rem(c, CORES)
    x, y = m // ny, lax.rem(m, ny)
    chain = c * members + m
    last = nz * CORES * members - 1
    has_prev, has_next = chain > 0, chain < last
    first_m, last_m = m == 0, m == members - 1
    prev = (jnp.where(first_m, c - 1, c), jnp.where(first_m, members - 1, m - 1))
    nxt = (jnp.where(last_m, c + 1, c), jnp.where(last_m, 0, m + 1))
    y_peers = [(c, x * ny + lax.rem(y + i, ny)) for i in range(1, ny)]
    x_peers = [(c, lax.rem(x + i, nx) * ny + y) for i in range(1, nx)]
    z_peers = [(lax.rem(z + i, nz) * CORES + core, m) for i in range(1, nz)]
    partner = (z * CORES + 1 - core, m)

    def copy(src, dst, ss, rs, device):
        return pltpu.make_async_remote_copy(
            src_ref=src, dst_ref=dst, send_sem=ss, recv_sem=rs, device_id=device, device_id_type=MESH
        )

    def take(ref, sem):
        pltpu.make_async_copy(ref, ref, sem).wait()

    barrier = pltpu.get_barrier_semaphore()
    peers = y_peers + x_peers + z_peers + [partner]
    for peer in peers:
        pl.semaphore_signal(barrier, inc=1, device_id=peer, device_id_type=MESH)

    @pl.when(has_prev)
    def _():
        pl.semaphore_signal(barrier, inc=1, device_id=prev, device_id_type=MESH)

    @pl.when(has_next)
    def _():
        pl.semaphore_signal(barrier, inc=1, device_id=nxt, device_id_type=MESH)

    oper_copy = pltpu.make_async_copy(oper_hbm, oper, oper_sem)
    oper_copy.start()

    own_basis[...] = jnp.zeros_like(own_basis)
    for k in range(modes):
        own_basis[k : k + 1, :] = basis_ref[k]
    for k in range(SUMS):
        ybuf[k, y] = jnp.zeros((2 * GROUP, LANES), F32)
        for core_id in range(CORES):
            zbuf[k, core_id, 0] = jnp.zeros((2 * GROUP, LANES), F32)
            zbuf[k, core_id, nz + 1] = jnp.zeros((2 * GROUP, LANES), F32)

    @pl.when(jnp.logical_not(has_prev))
    def _():
        nbr_basis[0] = jnp.zeros((GROUP, face), F32)
        for k in range(HALOS):
            halo[k, 0] = jnp.zeros((loads, face), F32)

    @pl.when(jnp.logical_not(has_next))
    def _():
        nbr_basis[1] = jnp.zeros((GROUP, face), F32)
        for k in range(HALOS):
            halo[k, 1] = jnp.zeros((loads, face), F32)

    coarse_size = coarse_ref.shape[0]
    row = lax.broadcasted_iota(jnp.int32, (SPAN, coarse_size), 0)
    entry = lax.broadcasted_iota(jnp.int32, (SPAN, coarse_size), 1)
    wanted = modes * (c - 1 + (row >> 3)) + (row & 7)
    pick = jnp.where((wanted == entry) & ((row & 7) < modes) & (row < 3 * GROUP), 1.0, 0.0)
    total_rows = CORES * nz * GROUP
    entry = lax.broadcasted_iota(jnp.int32, (coarse_size, total_rows), 0)
    col = lax.broadcasted_iota(jnp.int32, (coarse_size, total_rows), 1)
    col_core = jnp.where(col >= nz * GROUP, 1, 0)
    rest = col - nz * GROUP * col_core
    wanted = modes * (CORES * (rest >> 3) + col_core) + (rest & 7)
    place = jnp.where((wanted == entry) & ((rest & 7) < modes), 1.0, 0.0)
    coarse[...] = exact(exact(pick, coarse_ref[...]), place)

    def invert(t, carry):
        where = t * LANES + lax.broadcasted_iota(jnp.int32, (LANES, LANES), 0)
        found = jnp.zeros((LANES, LANES), F32)
        for u in range(chunks):
            here = (u * LANES + lax.broadcasted_iota(jnp.int32, (LANES, LANES), 1)).astype(F32)
            line = jnp.broadcast_to(index_ref[:, u * LANES : (u + 1) * LANES], (LANES, LANES))
            found = jnp.where(line == where, here, found)
        line = jnp.sum(found.T, axis=0, keepdims=True).astype(jnp.int32)
        inverse[:, pl.ds(pl.multiple_of(t * LANES, LANES), LANES)] = jnp.broadcast_to(
            line, (GROUP, LANES)
        )
        return carry

    lax.fori_loop(0, chunks, invert, 0)

    greetings = len(peers) + has_prev.astype(jnp.int32) + has_next.astype(jnp.int32)
    pl.semaphore_wait(barrier, greetings)

    def faces(src, dst, ss, rs):
        up = copy(src.at[:, pl.ds(face, face)], dst.at[0], ss.at[0], rs.at[0], nxt)
        down = copy(src.at[:, pl.ds(0, face)], dst.at[1], ss.at[1], rs.at[1], prev)
        return up, down

    def start_faces(src, dst, ss, rs):
        up, down = faces(src, dst, ss, rs)

        @pl.when(has_next)
        def _():
            up.start()

        @pl.when(has_prev)
        def _():
            down.start()

    def wait_faces(src, dst, ss, rs):
        up, down = faces(src, dst, ss, rs)

        @pl.when(has_prev)
        def _():
            up.wait_recv()

        @pl.when(has_next)
        def _():
            down.wait_recv()

    def drain_faces(src, dst, ss, rs):
        up, down = faces(src, dst, ss, rs)

        @pl.when(has_next)
        def _():
            up.wait_send()

        @pl.when(has_prev)
        def _():
            down.wait_send()

    def halo_args(k):
        src = load_ref if k == 0 else sent.at[k - 1]
        return src, halo.at[k], halo_s.at[k], halo_r.at[k]

    basis_args = (own_basis, nbr_basis, basis_s, basis_r)
    start_faces(*basis_args)
    wait_faces(*basis_args)
    low, high = nbr_basis[0], nbr_basis[1]
    at_first, at_last = first_m.astype(F32), last_m.astype(F32)
    span_f[...] = jnp.zeros_like(span_f)
    span_f[0:GROUP, 0:face] = low * at_first
    span_f[GROUP : 2 * GROUP, 0:face] = own_basis[:, 0:face] + low * (1.0 - at_first)
    span_f[GROUP : 2 * GROUP, face:slots] = own_basis[:, face:slots] + high * (1.0 - at_last)
    span_f[2 * GROUP : 3 * GROUP, face:slots] = high * at_last
    s_high, s_low = split(span_f[...])
    span_h[...] = s_high
    span_l[...] = s_low

    def restrict(v):
        v_high, v_low = split(v)
        both = nt(jnp.concatenate([span_h[...], span_l[...]], axis=0), v_high)
        return both[:SPAN] + both[SPAN:] + nt(span_h[...], v_low)

    def expand(amounts):
        turned = amounts.T
        a_high, a_low = split(turned)
        both = mm(jnp.concatenate([a_high, a_low], axis=0), span_h[...])
        return both[:loads] + both[loads:] + mm(a_high, span_l[...])

    def put_restricted(k, v):
        terms = restrict(v)
        ybuf[k, y, 0:GROUP, 0:loads] = terms[GROUP : 2 * GROUP]
        ybuf[k, y, GROUP : 2 * GROUP, :] = jnp.concatenate(
            [terms[0:GROUP], terms[2 * GROUP : 3 * GROUP]], axis=1
        )

    def reduce(k, rows, between):
        own = ybuf.at[k, y, 0:rows]
        for peer in y_peers:
            copy(own, own, y_s.at[k], y_r.at[k], peer).start()
        take(ybuf.at[k, 0 : ny - 1, 0:rows], y_r.at[k])
        total = ybuf[k, 0, 0:rows]
        for i in range(1, ny):
            total = total + ybuf[k, i, 0:rows]
        xbuf[k, x, 0:rows] = total
        own = xbuf.at[k, x, 0:rows]
        for peer in x_peers:
            copy(own, own, x_s.at[k], x_r.at[k], peer).start()
        between()
        take(xbuf.at[k, 0 : nx - 1, 0:rows], x_r.at[k])
        total = xbuf[k, 0, 0:rows]
        for i in range(1, nx):
            total = total + xbuf[k, i, 0:rows]
        zbuf[k, core, z + 1, 0:rows] = total
        own = zbuf.at[k, core, z + 1, 0:rows]
        for peer in z_peers:
            copy(own, own, z_s.at[k], z_r.at[k], peer).start()
        take(zbuf.at[k, 0, 1:nz, 0:rows], z_r.at[k])
        mine = zbuf.at[k, core, 1 : nz + 1, 0:rows]
        swap = copy(mine, mine, c_s.at[k], c_r.at[k], partner)
        swap.start()
        swap.wait_recv()

    def drain(k, rows):
        take(ybuf.at[k, 0 : ny - 1, 0:rows], y_s.at[k])
        take(xbuf.at[k, 0 : nx - 1, 0:rows], x_s.at[k])
        take(zbuf.at[k, 0, 1:nz, 0:rows], z_s.at[k])
        take(zbuf.at[k, 0, 1 : nz + 1, 0:rows], c_s.at[k])

    def amounts(k):
        def part(core_id, shift, rows, lanes):
            return zbuf[k, core_id, 1 + shift : 1 + shift + nz, rows : rows + GROUP, lanes : lanes + loads]

        even = part(0, 0, 0, 0) + part(1, 0, GROUP, 0) + part(1, -1, GROUP, LANES - loads)
        odd = part(1, 0, 0, 0) + part(0, 1, GROUP, 0) + part(0, 0, GROUP, LANES - loads)
        half = nz * GROUP
        totals = jnp.concatenate([even.reshape(half, loads), odd.reshape(half, loads)], axis=0)
        return exact(coarse[...], totals)

    def scalar_sum(k, line):
        total = zbuf[k, 0, 1, line : line + 1, 0:loads]
        for core_id in range(CORES):
            for i in range(nz):
                if core_id or i:
                    total = total + zbuf[k, core_id, 1 + i, line : line + 1, 0:loads]
        return total

    def row_sum(v):
        part = v[:, 0:LANES]
        for t in range(1, chunks):
            part = part + v[:, t * LANES : (t + 1) * LANES]
        return jnp.sum(part.T, axis=0, keepdims=True)

    def spread(line):
        column = jnp.broadcast_to(line, (LANES, loads)).T
        return jnp.concatenate([column] * chunks, axis=1)

    low_weight = jnp.where(has_prev, 0.5, 1.0).astype(F32)
    high_weight = jnp.where(has_next, 0.5, 1.0).astype(F32)

    def weighted(v):
        return jnp.concatenate([v[:, 0:face] * low_weight, v[:, face:slots] * high_weight], axis=1)

    def assembled(k, v):
        return jnp.concatenate([v[:, 0:face] + halo[k, 0], v[:, face:slots] + halo[k, 1]], axis=1)

    def precondition(w, out):
        scaled = weighted(w).astype(BF16)
        for n in range(nblock):
            cols = slice(n * block, (n + 1) * block)
            weight = low_weight if n < nblock // 2 else high_weight
            out[:, cols] = weight * mm(scaled[:, cols], blocks_ref[n])

    def permute(src, order, dst, scale=None):
        for t in range(chunks):
            cols = slice(t * LANES, (t + 1) * LANES)
            line = jnp.broadcast_to(order[0:1, cols], (loads, LANES))
            lane, chunk = line & (LANES - 1), line >> 7
            found = jnp.zeros((loads, LANES), F32)
            for u in range(chunks):
                seen = jnp.take_along_axis(
                    src[:, u * LANES : (u + 1) * LANES], lane, axis=1, mode="promise_in_bounds"
                )
                found = jnp.where(chunk == u, seen, found)
            dst[:, cols] = found if scale is None else found * scale

    softness = 1.0 / jnp.broadcast_to(stiff_ref[...], (loads, LANES))

    def nothing():
        pass

    def starter(k):
        return functools.partial(start_faces, *halo_args(k))

    put_restricted(0, load_ref[...])
    reduce(0, 2 * GROUP, starter(0))
    wait_faces(*halo_args(0))
    resid[...] = assembled(0, load_ref[...])
    amount_r = amounts(0)
    proj[...] = resid[...] - expand(amount_r)

    precondition(proj[...], sent.at[0])
    put_restricted(1, sent[0])
    reduce(1, 2 * GROUP, starter(1))
    wait_faces(*halo_args(1))
    search0[...] = assembled(1, sent[0]) - expand(amounts(1))

    permute(search0, inverse, temp)
    oper_copy.wait()
    temp[...] = mm(temp[...].astype(BF16), oper[...])
    permute(temp, index_ref, sent.at[1], softness)
    put_restricted(2, sent[1])
    ybuf[2, y, 6:7, 0:loads] = row_sum(weighted(proj[...]) * search0[...])
    ybuf[2, y, 7:8, 0:loads] = row_sum(search0[...] * sent[1])
    reduce(2, 2 * GROUP, starter(2))
    rho0, gamma0 = scalar_sum(2, 6), scalar_sum(2, 7)
    step0 = rho0 / gamma0
    amount_r = amount_r - step0 * amounts(2)
    wait_faces(*halo_args(2))
    image_q[...] = assembled(2, sent[1])
    resid[...] = resid[...] - spread(step0) * image_q[...]
    proj[...] = resid[...] - expand(amount_r)

    precondition(proj[...], sent.at[2])
    put_restricted(3, sent[2])
    reduce(3, 2 * GROUP, starter(3))
    wait_faces(*halo_args(3))
    search1[...] = assembled(3, sent[2]) - expand(amounts(3))

    permute(search1, inverse, temp)
    t_high, t_low = split(temp[...])
    both = mm(jnp.concatenate([t_high, t_low], axis=0), oper[...])
    temp[...] = both[:loads] + both[loads:]
    permute(temp, index_ref, sent.at[3], softness)
    ybuf[4, y, 0:1, 0:loads] = row_sum(weighted(proj[...]) * search1[...])
    ybuf[4, y, 1:2, 0:loads] = row_sum(search1[...] * sent[3])
    ybuf[4, y, 2:3, 0:loads] = row_sum(search1[...] * sent[1])
    reduce(4, GROUP, starter(4))
    rho1 = scalar_sum(4, 0)
    beta = rho1 / rho0
    gamma1 = scalar_sum(4, 1) + 2.0 * beta * scalar_sum(4, 2) + beta * beta * gamma0
    step1 = rho1 / gamma1
    wait_faces(*halo_args(4))
    beta_all, step1_all = spread(beta), spread(step1)
    direction = search1[...] + beta_all * search0[...]
    mult_out[...] = spread(step0) * search0[...] + step1_all * direction
    resid_out[...] = resid[...] - step1_all * (assembled(4, sent[3]) + beta_all * image_q[...])

    drain_faces(*basis_args)
    for k in range(HALOS):
        drain_faces(*halo_args(k))
    for k in range(SUMS):
        drain(k, 2 * GROUP if k < SUMS - 1 else GROUP)


def per_device(
    dual_load, dual_operator, index_map, stiffness, coarse_basis, dirichlet_blocks, coarse_inverse
):
    loads, face = dual_load.shape[2], dual_load.shape[4]
    slots = 2 * face
    modes = coarse_basis.shape[2]
    clusters, members = lax.axis_size("cluster"), lax.axis_size("member")
    nz, ny, nx = clusters // CORES, NY, members // NY
    vmem = pl.BlockSpec(memory_space=pltpu.VMEM)
    vector = pltpu.VMEM((loads, slots), F32)
    dma = pltpu.SemaphoreType.DMA
    mult, resid = pl.pallas_call(
        kernel,
        out_shape=[jax.ShapeDtypeStruct((loads, slots), F32)] * 2,
        in_specs=[vmem] * 6 + [pl.BlockSpec(memory_space=pl.ANY)],
        out_specs=[vmem] * 2,
        scratch_shapes=[
            pltpu.VMEM((slots, slots), BF16),
            pltpu.VMEM((GROUP, slots), F32),
            pltpu.VMEM((2, GROUP, face), F32),
            pltpu.VMEM((SPAN, slots), F32),
            pltpu.VMEM((SPAN, slots), BF16),
            pltpu.VMEM((SPAN, slots), BF16),
            pltpu.VMEM((SPAN, clusters * GROUP), F32),
            pltpu.VMEM((GROUP, slots), jnp.int32),
            pltpu.VMEM((HALOS, 2, loads, face), F32),
            pltpu.VMEM((HALOS - 1, loads, slots), F32),
            vector,
            vector,
            vector,
            vector,
            vector,
            vector,
            pltpu.VMEM((SUMS, ny, 2 * GROUP, LANES), F32),
            pltpu.VMEM((SUMS, nx, 2 * GROUP, LANES), F32),
            pltpu.VMEM((SUMS, CORES, nz + 2, 2 * GROUP, LANES), F32),
            dma,
            dma((2,)),
            dma((2,)),
            dma((HALOS, 2)),
            dma((HALOS, 2)),
        ]
        + [dma((SUMS,))] * 8,
        compiler_params=pltpu.CompilerParams(
            collective_id=0, has_side_effects=True, vmem_limit_bytes=56 * 2**20
        ),
        name="pcpg",
    )(
        dual_load.reshape(loads, slots),
        coarse_basis.reshape(modes, 1, slots),
        dirichlet_blocks.reshape(dirichlet_blocks.shape[2:]),
        coarse_inverse,
        index_map.reshape(1, slots),
        stiffness,
        dual_operator,
    )
    return mult.reshape(dual_load.shape), resid.reshape(dual_load.shape)


def solution(mesh):
    five = P("cluster", "member", None, None, None)
    in_specs = (
        five,
        P(),
        P("cluster", "member", None),
        P("cluster", "member"),
        P("cluster", "member", None, None),
        five,
        P(),
    )
    return jax.shard_map(
        per_device, mesh=mesh, in_specs=in_specs, out_specs=(five, five), check_vma=False
    )
```

time: 946 us -> 146 us (0.15)
  blocking collectives: 720 us -> 0 us
  Pallas kernels: 0 us -> 138 us
  starting transfers between devices: 86.3 us -> 0 us
  local copies, waits for them, and re-layouts: 59.7 us -> 6.54 us
  waiting for transfers between devices: 34.5 us -> 0 us
  matrix products: 25.8 us -> 0 us
  other arithmetic: 15.6 us -> 0 us
    psum x7 -> x0, blocking collectives: 564 us -> none  [the longest x3 329 us: inner(): lax.psum(jnp.sum(weights * left * right, axis=(1, 2)), ('cluster', 'membe...]
    all_gather x4 -> x0, blocking collectives: 156 us -> none  [project(): lax.all_gather(summed, 'cluster', axis=1, tiled=True)]
    pallas_call x0 -> x1, Pallas kernels: none -> 138 us  [per_device(): pl.pallas_call(kernel, out_shape=[jax.ShapeDtypeStruct((loads, slots), F3...]
    ppermute x18 -> x0, starting transfers between devices: 86.3 us -> none  [the longest x9 65 us: with_halo(): after = lax.ppermute(initial, axis, down)]
    gather x6 -> x0, local copies, waits for them, and re-layouts: 35.2 us -> none  [the longest x4 19.1 us: per_device(): jnp.take(product, ordering, axis=1)]
    ppermute x18 -> x0, waiting for transfers between devices: 34.5 us -> none  [the longest x9 24.2 us: with_halo(): after = lax.ppermute(initial, axis, down)]
    dot_general x16 -> x0, matrix products: 25.8 us -> none  [the longest x2 14.4 us: per_device(): jnp.dot(local_order, dual_operator, preferred_element_type=jnp.float32)]
  transfers between devices with their start and end apart: 18 -> 0, of which waited for: 15 -> 0; matrix products, arithmetic and copies ran while one was open for 2% -> 0% of each run, Pallas kernels for 0% -> 0%
where the time goes in v1:
time: 146 us
  Pallas kernels  138 us (95%)
  local copies, waits for them, and re-layouts  6.54 us (4%)
    pallas_call x1, Pallas kernels, per_device(): pl.pallas_call(kernel, out_shape=[jax.ShapeDtypeStruct((loads, slots), F3...  138 us
    reshape x2, local copies, waits for them, and re-layouts, per_device(): return (mult.reshape(dual_load.shape), resid.reshape(dual_load.shape))  4.55 us

profile of v1, /device:TPU:1, one launch (start us, length us, event | category | flops | bytes accessed | tf_op | source)
XLA Modules:
  0.0 146.2 jit_solution(6449853093560305692)
XLA Ops:
  1.3 2.0 %copy.9 = f32[8,8,2,1024]{3,1,2,0:T(8,128)} copy(f32[8,8,2,1024]{3,2,1,0:T(2,128)} %bitcast.8) | data formatting | bytes 1048576
  3.3 138.3 %pcpg.1 = (f32[64,2048]{1,0:T(8,128)}, f32[64,2048]{1,0:T(8,128)}) custom-call(f32[64,2048]{1,0:T(8,128)} %bitcast.6, f32[6,1,2048]{2,1,0:T(1,128)} %bitcast.9, bf16[16,128,128]{2,1,0:T(8,128)(2,1)} %bitcast.7, f32[144,144]{1,0:T(8,128)} %coarse_ref.1, s32[1,2048]{1,0:T(1,128)} %bitcast.10, f32[1,1]{1,0:T(1,128)S(6)} %copy.10.stiff_ref, ...), custom_call_target="tpu_custom_call" | custom-call | tf_op jit(solution)/shard_map/pcpg/pallas_call | solution.py:426
  141.6 2.3 %reshape.26 = f32[1,1,64,2,1024]{4,3,2,1,0:T(2,128)} reshape(f32[64,2048]{1,0:T(8,128)} %get-tuple-element.4) | data formatting | bytes 1048576 | tf_op jit(solution)/shard_map/reshape | solution.py:471
  143.9 2.3 %reshape.27 = f32[1,1,64,2,1024]{4,3,2,1,0:T(2,128)} reshape(f32[64,2048]{1,0:T(8,128)} %get-tuple-element.5) | data formatting | bytes 1048576 | tf_op jit(solution)/shard_map/reshape | solution.py:471

commit v2 on v1

v2 whole, which is shorter than its diff:
```python
import jax
import jax.numpy as jnp
from jax import lax
from jax.experimental import pallas as pl
from jax.experimental.pallas import tpu as pltpu
from jax.sharding import PartitionSpec as P

MESH = pl.DeviceIdType.MESH
NY = 8
CORES = 2
GROUP = 8
SPAN = 32
LANES = 128
HALOS = 5
SUMS = 3
WIDE = 3 * GROUP
F32 = jnp.float32
BF16 = jnp.bfloat16


def nt(a, b):
    return lax.dot_general(a, b, (((1,), (1,)), ((), ())), preferred_element_type=F32)


def mm(a, b):
    return jnp.dot(a, b, preferred_element_type=F32)


def exact(a, b):
    return jnp.dot(a, b, precision=lax.Precision.HIGHEST, preferred_element_type=F32)


def split(v):
    high = v.astype(BF16)
    return high, (v - high.astype(F32)).astype(BF16)


def kernel(
    basis_ref,
    coarse_ref,
    index_ref,
    stiff_ref,
    load_hbm,
    blocks_hbm,
    oper_hbm,
    mult_out,
    resid_out,
    raw,
    blocks,
    oper,
    load,
    own_basis,
    nbr_basis,
    span_f,
    span_h,
    span_l,
    order_h,
    order_l,
    wide,
    coarse,
    amount,
    gram,
    inverse,
    halo,
    halo_span,
    sent,
    sent_span,
    resid,
    proj,
    search0,
    search1,
    image_q,
    turned0,
    turned1,
    image0,
    image1,
    ybuf,
    xbuf,
    zbuf,
    local_sem,
    basis_s,
    basis_r,
    span_s,
    span_r,
    halo_s,
    halo_r,
    y_s,
    y_r,
    x_s,
    x_r,
    z_s,
    z_r,
    c_s,
    c_r,
):
    loads, slots = load.shape
    face = slots // 2
    chunks = slots // LANES
    modes = basis_ref.shape[0]
    nblock, block = blocks.shape[:2]
    nz = zbuf.shape[1] - 2
    nx = xbuf.shape[1]
    ny = ybuf.shape[1]
    members = nx * ny
    clusters = nz * CORES
    c = lax.axis_index("cluster")
    m = lax.axis_index("member")
    z, core = c // CORES, lax.rem(c, CORES)
    x, y = m // ny, lax.rem(m, ny)
    chain = c * members + m
    last = clusters * members - 1
    has_prev, has_next = chain > 0, chain < last
    first_m, last_m = m == 0, m == members - 1
    prev = (jnp.where(first_m, c - 1, c), jnp.where(first_m, members - 1, m - 1))
    nxt = (jnp.where(last_m, c + 1, c), jnp.where(last_m, 0, m + 1))
    y_peers = [(c, x * ny + lax.rem(y + i, ny)) for i in range(1, ny)]
    x_peers = [(c, lax.rem(x + i, nx) * ny + y) for i in range(1, nx)]
    z_peers = [(lax.rem(z + i, nz) * CORES + core, m) for i in range(1, nz)]
    partner = (z * CORES + 1 - core, m)

    def copy(src, dst, ss, rs, device):
        return pltpu.make_async_remote_copy(
            src_ref=src, dst_ref=dst, send_sem=ss, recv_sem=rs, device_id=device, device_id_type=MESH
        )

    def take(ref, sem):
        pltpu.make_async_copy(ref, ref, sem).wait()

    barrier = pltpu.get_barrier_semaphore()
    peers = z_peers + y_peers + x_peers + [partner]
    for peer in peers:
        pl.semaphore_signal(barrier, inc=1, device_id=peer, device_id_type=MESH)

    @pl.when(has_prev)
    def _():
        pl.semaphore_signal(barrier, inc=1, device_id=prev, device_id_type=MESH)

    @pl.when(has_next)
    def _():
        pl.semaphore_signal(barrier, inc=1, device_id=nxt, device_id_type=MESH)

    raw_copy = pltpu.make_async_copy(load_hbm, raw, local_sem.at[0])
    blocks_copy = pltpu.make_async_copy(blocks_hbm, blocks, local_sem.at[1])
    oper_copy = pltpu.make_async_copy(oper_hbm, oper, local_sem.at[2])
    raw_copy.start()
    blocks_copy.start()
    oper_copy.start()

    own_basis[...] = jnp.zeros_like(own_basis)
    for k in range(modes):
        own_basis[k : k + 1, :] = basis_ref[k]
    zero_tile = jnp.zeros((WIDE, LANES), F32)
    for k in range(SUMS):
        ybuf[k, y] = zero_tile
        for core_id in range(CORES):
            zbuf[k, 0, core_id] = zero_tile
            zbuf[k, nz + 1, core_id] = zero_tile
    amount[...] = jnp.zeros_like(amount)

    @pl.when(jnp.logical_not(has_prev))
    def _():
        nbr_basis[0] = jnp.zeros((GROUP, face), F32)
        halo_span[0] = jnp.zeros((SPAN, face), F32)
        for k in range(HALOS):
            halo[k, 0] = jnp.zeros((loads, face), F32)

    @pl.when(jnp.logical_not(has_next))
    def _():
        nbr_basis[1] = jnp.zeros((GROUP, face), F32)
        halo_span[1] = jnp.zeros((SPAN, face), F32)
        for k in range(HALOS):
            halo[k, 1] = jnp.zeros((loads, face), F32)

    raw_copy.wait()
    for f in range(2):
        for t in range(chunks // 2):
            start = f * face + t * LANES
            load[:, start : start + LANES] = raw[pl.ds(2 * t + f, loads, stride=chunks), :]

    coarse_size = coarse_ref.shape[0]
    total_rows = clusters * GROUP

    def placed(row, entry):
        return jnp.where((modes * (row >> 3) + (row & 7) == entry) & ((row & 7) < modes), 1.0, 0.0)

    shape = (total_rows, coarse_size)
    down = placed(lax.broadcasted_iota(jnp.int32, shape, 0), lax.broadcasted_iota(jnp.int32, shape, 1))
    shape = (coarse_size, total_rows)
    across = placed(
        lax.broadcasted_iota(jnp.int32, shape, 1), lax.broadcasted_iota(jnp.int32, shape, 0)
    )
    coarse[...] = exact(exact(down, coarse_ref[...]), across)

    def invert(t, carry):
        where = t * LANES + lax.broadcasted_iota(jnp.int32, (LANES, LANES), 0)
        found = jnp.zeros((LANES, LANES), F32)
        for u in range(chunks):
            here = (u * LANES + lax.broadcasted_iota(jnp.int32, (LANES, LANES), 1)).astype(F32)
            line = jnp.broadcast_to(index_ref[:, u * LANES : (u + 1) * LANES], (LANES, LANES))
            found = jnp.where(line == where, here, found)
        line = jnp.sum(found.T, axis=0, keepdims=True).astype(jnp.int32)
        inverse[:, pl.ds(pl.multiple_of(t * LANES, LANES), LANES)] = jnp.broadcast_to(
            line, (GROUP, LANES)
        )
        return carry

    lax.fori_loop(0, chunks, invert, 0)
    blocks_copy.wait()

    greetings = len(peers) + has_prev.astype(jnp.int32) + has_next.astype(jnp.int32)
    pl.semaphore_wait(barrier, greetings)

    def faces(src, dst, ss, rs):
        up = copy(src.at[:, pl.ds(face, face)], dst.at[0], ss.at[0], rs.at[0], nxt)
        down = copy(src.at[:, pl.ds(0, face)], dst.at[1], ss.at[1], rs.at[1], prev)
        return up, down

    def start_faces(args):
        up, down = faces(*args)

        @pl.when(has_next)
        def _():
            up.start()

        @pl.when(has_prev)
        def _():
            down.start()

    def wait_faces(args):
        up, down = faces(*args)

        @pl.when(has_prev)
        def _():
            up.wait_recv()

        @pl.when(has_next)
        def _():
            down.wait_recv()

    def drain_faces(args):
        up, down = faces(*args)

        @pl.when(has_next)
        def _():
            up.wait_send()

        @pl.when(has_prev)
        def _():
            down.wait_send()

    basis_args = (own_basis, nbr_basis, basis_s, basis_r)
    span_args = (sent_span, halo_span, span_s, span_r)
    halo_args = [
        (load if k == 0 else sent.at[k - 1], halo.at[k], halo_s.at[k], halo_r.at[k])
        for k in range(HALOS)
    ]

    def reduce(k, rows, after_y, after_x, after_z):
        own = ybuf.at[k, y, 0:rows]
        for peer in y_peers:
            copy(own, own, y_s.at[k], y_r.at[k], peer).start()
        after_y()
        take(ybuf.at[k, 0 : ny - 1, 0:rows], y_r.at[k])
        total = ybuf[k, 0, 0:rows]
        for i in range(1, ny):
            total = total + ybuf[k, i, 0:rows]
        xbuf[k, x, 0:rows] = total
        own = xbuf.at[k, x, 0:rows]
        for peer in x_peers:
            copy(own, own, x_s.at[k], x_r.at[k], peer).start()
        after_x()
        take(xbuf.at[k, 0 : nx - 1, 0:rows], x_r.at[k])
        total = xbuf[k, 0, 0:rows]
        for i in range(1, nx):
            total = total + xbuf[k, i, 0:rows]
        zbuf[k, z + 1, core, 0:rows] = total
        own = zbuf.at[k, z + 1, core, 0:rows]
        for peer in z_peers:
            copy(own, own, z_s.at[k], z_r.at[k], peer).start()
        after_z()
        take(zbuf.at[k, 1:nz, 0, 0:rows], z_r.at[k])
        mine = zbuf.at[k, 1 : nz + 1, core, 0:rows]
        swap = copy(mine, mine, c_s.at[k], c_r.at[k], partner)
        swap.start()
        swap.wait_recv()

    def drain(k, rows):
        take(ybuf.at[k, 0 : ny - 1, 0:rows], y_s.at[k])
        take(xbuf.at[k, 0 : nx - 1, 0:rows], x_s.at[k])
        take(zbuf.at[k, 1:nz, 0, 0:rows], z_s.at[k])
        take(zbuf.at[k, 1 : nz + 1, 0, 0:rows], c_s.at[k])

    def gathered(k):
        return zbuf[k].reshape(CORES * (nz + 2), WIDE, LANES)

    def fold(parts):
        total = (
            parts[2 : 2 + clusters, GROUP : 2 * GROUP]
            + parts[3 : 3 + clusters, 0:GROUP]
            + parts[1 : 1 + clusters, 2 * GROUP : WIDE]
        )
        return total.reshape(total_rows, LANES)

    def solve(totals):
        amounts = exact(coarse[...], totals)
        amount[GROUP : GROUP + total_rows, 0:loads] = amounts
        return amount[pl.ds(pl.multiple_of(GROUP * c, GROUP), SPAN), 0:loads]

    def gram_amount():
        parts = [
            exact(gram[j], amount[GROUP * j : GROUP * j + SPAN, 0:loads]) for j in range(clusters)
        ]
        rows = []
        for j in range(clusters):
            line = parts[j][GROUP : 2 * GROUP]
            if j + 1 < clusters:
                line = line + parts[j + 1][0:GROUP]
            if j > 0:
                line = line + parts[j - 1][2 * GROUP : WIDE]
            rows.append(line)
        return jnp.concatenate(rows, axis=0)

    def restrict(high, low, v):
        rows = high.shape[0]
        v_high, v_low = split(v)
        both = nt(jnp.concatenate([high, low], axis=0), v_high)
        return both[:rows] + both[rows:] + nt(high, v_low)

    def expand(amounts, rows):
        a_high, a_low = split(amounts.T)
        both = mm(jnp.concatenate([a_high, a_low], axis=0), span_h[0:rows])
        return both[:loads] + both[loads:] + mm(a_high, span_l[0:rows])

    def row_sum(v):
        part = v[:, 0:LANES]
        for t in range(1, chunks):
            part = part + v[:, t * LANES : (t + 1) * LANES]
        return jnp.sum(part.T, axis=0, keepdims=True)

    def spread(line):
        column = jnp.broadcast_to(line, (LANES, loads)).T
        return jnp.concatenate([column] * chunks, axis=1)

    low_weight = jnp.where(has_prev, 0.5, 1.0).astype(F32)
    high_weight = jnp.where(has_next, 0.5, 1.0).astype(F32)

    def weighted(v):
        return jnp.concatenate([v[:, 0:face] * low_weight, v[:, face:slots] * high_weight], axis=1)

    def assembled(k, v):
        return jnp.concatenate([v[:, 0:face] + halo[k, 0], v[:, face:slots] + halo[k, 1]], axis=1)

    def precondition(v, out, parts=2):
        rows = v.shape[0]
        pair = jnp.concatenate(split(v)[:parts], axis=0)
        for n in range(nblock):
            cols = slice(n * block, (n + 1) * block)
            weight = low_weight if n < nblock // 2 else high_weight
            both = mm(pair[:, cols], blocks[n])
            if parts == 2:
                both = both[:rows] + both[rows:]
            out[:, cols] = (weight * weight) * both

    def permute(src, order, dst):
        rows = src.shape[0]
        for t in range(chunks):
            cols = slice(t * LANES, (t + 1) * LANES)
            line = jnp.broadcast_to(order[0:1, cols], (rows, LANES))
            lane, chunk = line & (LANES - 1), line >> 7
            found = jnp.zeros((rows, LANES), F32)
            for u in range(chunks):
                seen = jnp.take_along_axis(
                    src[:, u * LANES : (u + 1) * LANES], lane, axis=1, mode="promise_in_bounds"
                )
                found = jnp.where(chunk == u, seen, found)
            dst[:, cols] = found

    softness = 1.0 / jnp.broadcast_to(stiff_ref[...], (loads, LANES))
    softness = jnp.concatenate([softness] * chunks, axis=1)

    def nothing():
        pass

    start_faces(basis_args)
    start_faces(halo_args[0])
    wait_faces(basis_args)
    low, high = nbr_basis[0], nbr_basis[1]
    at_first, at_last = first_m.astype(F32), last_m.astype(F32)
    span_f[...] = jnp.zeros_like(span_f)
    span_f[0:GROUP, 0:face] = low * at_first
    span_f[GROUP : 2 * GROUP, 0:face] = own_basis[:, 0:face] + low * (1.0 - at_first)
    span_f[GROUP : 2 * GROUP, face:slots] = own_basis[:, face:slots] + high * (1.0 - at_last)
    span_f[2 * GROUP : WIDE, face:slots] = high * at_last
    s_high, s_low = split(span_f[...])
    span_h[0:SPAN] = s_high
    span_l[0:SPAN] = s_low
    precondition(span_f[...], sent_span)
    own_gram = restrict(span_h[0:SPAN], span_l[0:SPAN], sent_span[...])
    permute(span_f, inverse, wide)
    s_high, s_low = split(wide[...])
    order_h[0:SPAN] = s_high
    order_l[0:SPAN] = s_low

    wait_faces(halo_args[0])
    resid[...] = assembled(0, load[...])
    precondition(resid[...], sent.at[0])

    terms = restrict(span_h[0:SPAN], span_l[0:SPAN], sent[0])
    o_high, o_low = split(jnp.concatenate([own_basis[...], jnp.zeros_like(own_basis)], axis=0))
    own_terms = restrict(o_high, o_low, resid[...])
    ybuf[0, y, 0:GROUP, :] = jnp.concatenate(
        [terms[0:GROUP], own_gram[0:GROUP], own_gram[GROUP : 2 * GROUP]], axis=1
    )
    ybuf[0, y, GROUP : 2 * GROUP, :] = jnp.concatenate(
        [terms[GROUP : 2 * GROUP], own_terms[0:GROUP]], axis=1
    )
    ybuf[0, y, 2 * GROUP : WIDE, 0:loads] = terms[2 * GROUP : WIDE]
    ybuf[0, y, 2 * GROUP : WIDE, loads : loads + SPAN] = own_gram[2 * GROUP : WIDE]

    def assemble_span():
        wait_faces(span_args)
        low, high = halo_span[0], halo_span[1]
        none = jnp.zeros((GROUP, face), F32)
        low_moved = jnp.concatenate([low[GROUP:SPAN], none], axis=0)
        high_moved = jnp.concatenate([none, high[0 : SPAN - GROUP]], axis=0)
        low = jnp.where(first_m, low_moved, low)
        high = jnp.where(last_m, high_moved, high)
        wide[:, 0:face] = sent_span[:, 0:face] + low
        wide[:, face:slots] = sent_span[:, face:slots] + high
        t_high, t_low = split(wide[...])
        span_h[SPAN : 2 * SPAN] = t_high
        span_l[SPAN : 2 * SPAN] = t_low
        permute(wide, inverse, span_f)
        t_high, t_low = split(span_f[...])
        order_h[SPAN : 2 * SPAN] = t_high
        order_l[SPAN : 2 * SPAN] = t_low

    def start_first():
        start_faces(span_args)
        start_faces(halo_args[1])

    reduce(0, WIDE, nothing, start_first, assemble_span)
    parts = gathered(0)
    for j in range(clusters):
        gram[j] = jnp.concatenate(
            [
                parts[j + 2, 0:GROUP, loads : loads + SPAN],
                parts[j + 2, 0:GROUP, loads + SPAN : LANES],
                parts[j + 2, 2 * GROUP : WIDE, loads : loads + SPAN],
            ],
            axis=0,
        )
    totals = parts[2 : 2 + clusters, GROUP : 2 * GROUP, LANES - loads : LANES]
    amount_r = solve(totals.reshape(total_rows, loads))
    reduced = fold(parts)[:, 0:loads] - gram_amount()
    amount_y = solve(reduced)
    wait_faces(halo_args[1])
    search0[...] = assembled(1, sent[0]) - expand(
        jnp.concatenate([amount_y, amount_r], axis=0), 2 * SPAN
    )
    proj[...] = resid[...] - expand(amount_r, SPAN)

    permute(search0, inverse, turned0)
    oper_copy.wait()
    image0[...] = softness * mm(turned0[...].astype(BF16), oper[...])
    terms = restrict(order_h[...], order_l[...], image0[...])
    ybuf[1, y] = jnp.concatenate([terms[0:WIDE], terms[SPAN : SPAN + WIDE]], axis=1)
    ybuf[1, y, 2 * GROUP - 2 : 2 * GROUP - 1, 0:loads] = row_sum(weighted(proj[...]) * search0[...])
    ybuf[1, y, 2 * GROUP - 1 : 2 * GROUP, 0:loads] = row_sum(turned0[...] * image0[...])
    reduce(
        1,
        WIDE,
        lambda: permute(image0, index_ref, sent.at[1]),
        lambda: start_faces(halo_args[2]),
        nothing,
    )
    parts = gathered(1)
    sums = jnp.sum(parts[2 : 2 + clusters, GROUP : 2 * GROUP, 0:loads], axis=0)
    rho0, gamma0 = sums[GROUP - 2 : GROUP - 1], sums[GROUP - 1 : GROUP]
    step0 = rho0 / gamma0
    totals = fold(parts)
    amount_r = amount_r - step0 * solve(totals[:, 0:loads])
    reduced = reduced - step0 * (totals[:, LANES - loads : LANES] - gram_amount())
    wait_faces(halo_args[2])
    image_q[...] = assembled(2, sent[1])
    resid[...] = resid[...] - spread(step0) * image_q[...]
    proj[...] = resid[...] - expand(amount_r, SPAN)
    precondition(proj[...], sent.at[2], 1)
    start_faces(halo_args[3])
    amount_y = solve(reduced)
    spread_y = expand(amount_y, SPAN)
    wait_faces(halo_args[3])
    search1[...] = assembled(3, sent[2]) - spread_y

    permute(search1, inverse, turned1)
    t_high, t_low = split(turned1[...])
    both = mm(jnp.concatenate([t_high, t_low], axis=0), oper[...])
    image1[...] = softness * (both[:loads] + both[loads:])
    ybuf[2, y, 0:1, 0:loads] = row_sum(weighted(proj[...]) * search1[...])
    ybuf[2, y, 1:2, 0:loads] = row_sum(turned1[...] * image1[...])
    ybuf[2, y, 2:3, 0:loads] = row_sum(turned1[...] * image0[...])
    reduce(
        2,
        GROUP,
        lambda: permute(image1, index_ref, sent.at[3]),
        lambda: start_faces(halo_args[4]),
        nothing,
    )
    sums = zbuf[2, 1, 0, 0:GROUP, 0:loads]
    for j in range(1, clusters):
        sums = sums + zbuf[2, 1 + j // CORES, j % CORES, 0:GROUP, 0:loads]
    rho1 = sums[0:1]
    beta = rho1 / rho0
    gamma1 = sums[1:2] + 2.0 * beta * sums[2:3] + beta * beta * gamma0
    step1 = rho1 / gamma1
    wait_faces(halo_args[4])
    beta_all, step0_all, step1_all = (spread(v)[:, 0:LANES] for v in (beta, step0, step1))
    for f in range(2):
        for t in range(chunks // 2):
            cols = slice(f * face + t * LANES, f * face + (t + 1) * LANES)
            near = slice(t * LANES, (t + 1) * LANES)
            rows = pl.ds(2 * t + f, loads, stride=chunks)
            first = search0[:, cols]
            direction = search1[:, cols] + beta_all * first
            mult_out[rows, :] = step0_all * first + step1_all * direction
            image = sent[3, :, cols] + halo[4, f, :, near] + beta_all * image_q[:, cols]
            resid_out[rows, :] = resid[:, cols] - step1_all * image

    drain_faces(basis_args)
    drain_faces(span_args)
    for k in range(HALOS):
        drain_faces(halo_args[k])
    for k in range(SUMS):
        drain(k, WIDE if k < SUMS - 1 else GROUP)


def per_device(
    dual_load, dual_operator, index_map, stiffness, coarse_basis, dirichlet_blocks, coarse_inverse
):
    loads, face = dual_load.shape[2], dual_load.shape[4]
    slots = 2 * face
    modes = coarse_basis.shape[2]
    clusters, members = lax.axis_size("cluster"), lax.axis_size("member")
    nz, ny, nx = clusters // CORES, NY, members // NY
    blocks_shape = dirichlet_blocks.shape[2:]
    vmem = pl.BlockSpec(memory_space=pltpu.VMEM)
    in_place = pl.BlockSpec(memory_space=pl.ANY)
    vector = pltpu.VMEM((loads, slots), F32)
    span = pltpu.VMEM((SPAN, slots), F32)
    spans = pltpu.VMEM((2 * SPAN, slots), BF16)
    dma = pltpu.SemaphoreType.DMA
    rows = loads * slots // LANES
    lines = (loads, face // LANES, 2, LANES)
    load = dual_load.reshape(loads, 2, face // LANES, LANES).transpose(0, 2, 1, 3)
    outs = pl.pallas_call(
        kernel,
        out_shape=[jax.ShapeDtypeStruct((rows, LANES), F32)] * 2,
        in_specs=[vmem] * 4 + [in_place] * 3,
        out_specs=[vmem] * 2,
        scratch_shapes=[
            pltpu.VMEM((rows, LANES), F32),
            pltpu.VMEM(blocks_shape, BF16),
            pltpu.VMEM((slots, slots), BF16),
            vector,
            pltpu.VMEM((GROUP, slots), F32),
            pltpu.VMEM((2, GROUP, face), F32),
            span,
            spans,
            spans,
            spans,
            spans,
            span,
            pltpu.VMEM((clusters * GROUP, clusters * GROUP), F32),
            pltpu.VMEM(((clusters + 3) * GROUP, LANES), F32),
            pltpu.VMEM((clusters, WIDE, SPAN), F32),
            pltpu.VMEM((GROUP, slots), jnp.int32),
            pltpu.VMEM((HALOS, 2, loads, face), F32),
            pltpu.VMEM((2, SPAN, face), F32),
            pltpu.VMEM((HALOS - 1, loads, slots), F32),
            span,
        ]
        + [vector] * 9
        + [
            pltpu.VMEM((SUMS, ny, WIDE, LANES), F32),
            pltpu.VMEM((SUMS, nx, WIDE, LANES), F32),
            pltpu.VMEM((SUMS, nz + 2, CORES, WIDE, LANES), F32),
            dma((3,)),
            dma((2,)),
            dma((2,)),
            dma((2,)),
            dma((2,)),
            dma((HALOS, 2)),
            dma((HALOS, 2)),
        ]
        + [dma((SUMS,))] * 8,
        compiler_params=pltpu.CompilerParams(
            collective_id=0, has_side_effects=True, vmem_limit_bytes=56 * 2**20
        ),
        name="pcpg",
    )(
        coarse_basis.reshape(modes, 1, slots),
        coarse_inverse,
        index_map.reshape(1, slots),
        stiffness,
        load.reshape(rows, LANES),
        dirichlet_blocks.reshape(blocks_shape),
        dual_operator,
    )
    mult, resid = (out.reshape(lines).transpose(0, 2, 1, 3).reshape(dual_load.shape) for out in outs)
    return mult, resid


def solution(mesh):
    five = P("cluster", "member", None, None, None)
    in_specs = (
        five,
        P(),
        P("cluster", "member", None),
        P("cluster", "member"),
        P("cluster", "member", None, None),
        five,
        P(),
    )
    return jax.shard_map(
        per_device, mesh=mesh, in_specs=in_specs, out_specs=(five, five), check_vma=False
    )
```

time: 146 us -> 117 us (0.80)
  Pallas kernels: 138 us -> 111 us
  local copies, waits for them, and re-layouts: 6.54 us -> 3.74 us
    pallas_call x1, Pallas kernels: 138 us -> 111 us  [per_device(): pl.pallas_call(kernel, out_shape=[jax.ShapeDtypeStruct((rows, LANES), F32...]
    reshape x2 -> x0, local copies, waits for them, and re-layouts: 4.55 us -> none  [per_device(): return (mult.reshape(dual_load.shape), resid.reshape(dual_load.shape))]
    unnamed x1 -> x2, local copies, waits for them, and re-layouts: 2 us -> 3.74 us
where the time goes in v2:
time: 117 us; the launch traced here: 116 us
  Pallas kernels  111 us (95%)
  local copies, waits for them, and re-layouts  3.74 us (3%)
  between operations  1.29 us (1%)
    pallas_call x1, Pallas kernels, per_device(): pl.pallas_call(kernel, out_shape=[jax.ShapeDtypeStruct((rows, LANES), F32...  111 us
    unnamed x2, local copies, waits for them, and re-layouts  3.74 us

profile of v2, /device:TPU:1, one launch (start us, length us, event | category | flops | bytes accessed | tf_op | source)
XLA Modules:
  0.0 116.4 jit_solution(13865438933016228222)
XLA Ops:
  1.3 111.4 %pcpg.1 = (f32[1024,128]{1,0:T(8,128)}, f32[1024,128]{1,0:T(8,128)}) custom-call(f32[6,1,2048]{2,1,0:T(1,128)} %bitcast.22, f32[144,144]{1,0:T(8,128)} %coarse_ref.1, s32[1,2048]{1,0:T(1,128)} %bitcast.23, f32[1,1]{1,0:T(1,128)S(6)} %copy.14.stiff_ref, f32[1024,128]{1,0:T(8,128)} %bitcast.18, bf16[16,128,128]{2,1,0:T(8,128)(2,1)} %bitcast.19, ...), custom_call_target="tpu_custom_call" | custom-call | tf_op jit(solution)/shard_map/pcpg/pallas_call | solution.py:555
  112.7 1.9 %copy.15 = f32[1,1,64,2,1024]{4,3,2,1,0:T(2,128)} copy(f32[1,1,64,2,1024]{4,3,2,1,0:T(2,128)} %bitcast.21) | data formatting | bytes 1048576
  114.6 1.9 %copy.16 = f32[1,1,64,2,1024]{4,3,2,1,0:T(2,128)} copy(f32[1,1,64,2,1024]{4,3,2,1,0:T(2,128)} %bitcast.20) | data formatting | bytes 1048576

commit v3 on v2

--- a/solution.py
+++ b/solution.py
@@ -149,63 +149,11 @@
     own_basis[...] = jnp.zeros_like(own_basis)
     for k in range(modes):
         own_basis[k : k + 1, :] = basis_ref[k]
-    zero_tile = jnp.zeros((WIDE, LANES), F32)
-    for k in range(SUMS):
-        ybuf[k, y] = zero_tile
-        for core_id in range(CORES):
-            zbuf[k, 0, core_id] = zero_tile
-            zbuf[k, nz + 1, core_id] = zero_tile
-    amount[...] = jnp.zeros_like(amount)
-
-    @pl.when(jnp.logical_not(has_prev))
-    def _():
-        nbr_basis[0] = jnp.zeros((GROUP, face), F32)
-        halo_span[0] = jnp.zeros((SPAN, face), F32)
-        for k in range(HALOS):
-            halo[k, 0] = jnp.zeros((loads, face), F32)
-
-    @pl.when(jnp.logical_not(has_next))
-    def _():
-        nbr_basis[1] = jnp.zeros((GROUP, face), F32)
-        halo_span[1] = jnp.zeros((SPAN, face), F32)
-        for k in range(HALOS):
-            halo[k, 1] = jnp.zeros((loads, face), F32)
-
     raw_copy.wait()
     for f in range(2):
         for t in range(chunks // 2):
             start = f * face + t * LANES
             load[:, start : start + LANES] = raw[pl.ds(2 * t + f, loads, stride=chunks), :]
-
-    coarse_size = coarse_ref.shape[0]
-    total_rows = clusters * GROUP
-
-    def placed(row, entry):
-        return jnp.where((modes * (row >> 3) + (row & 7) == entry) & ((row & 7) < modes), 1.0, 0.0)
-
-    shape = (total_rows, coarse_size)
-    down = placed(lax.broadcasted_iota(jnp.int32, shape, 0), lax.broadcasted_iota(jnp.int32, shape, 1))
-    shape = (coarse_size, total_rows)
-    across = placed(
-        lax.broadcasted_iota(jnp.int32, shape, 1), lax.broadcasted_iota(jnp.int32, shape, 0)
-    )
-    coarse[...] = exact(exact(down, coarse_ref[...]), across)
-
-    def invert(t, carry):
-        where = t * LANES + lax.broadcasted_iota(jnp.int32, (LANES, LANES), 0)
-        found = jnp.zeros((LANES, LANES), F32)
-        for u in range(chunks):
-            here = (u * LANES + lax.broadcasted_iota(jnp.int32, (LANES, LANES), 1)).astype(F32)
-            line = jnp.broadcast_to(index_ref[:, u * LANES : (u + 1) * LANES], (LANES, LANES))
-            found = jnp.where(line == where, here, found)
-        line = jnp.sum(found.T, axis=0, keepdims=True).astype(jnp.int32)
-        inverse[:, pl.ds(pl.multiple_of(t * LANES, LANES), LANES)] = jnp.broadcast_to(
-            line, (GROUP, LANES)
-        )
-        return carry
-
-    lax.fori_loop(0, chunks, invert, 0)
-    blocks_copy.wait()
 
     greetings = len(peers) + has_prev.astype(jnp.int32) + has_next.astype(jnp.int32)
     pl.semaphore_wait(barrier, greetings)
@@ -302,14 +250,18 @@
         return total.reshape(total_rows, LANES)
 
     def solve(totals):
-        amounts = exact(coarse[...], totals)
+        t_high, t_low = split(totals)
+        both = mm(coarse[...], t_high)
+        amounts = both[:total_rows] + both[total_rows:] + mm(coarse[0:total_rows], t_low)
         amount[GROUP : GROUP + total_rows, 0:loads] = amounts
         return amount[pl.ds(pl.multiple_of(GROUP * c, GROUP), SPAN), 0:loads]
 
     def gram_amount():
-        parts = [
-            exact(gram[j], amount[GROUP * j : GROUP * j + SPAN, 0:loads]) for j in range(clusters)
-        ]
+        parts = []
+        for j in range(clusters):
+            a_high, a_low = split(amount[GROUP * j : GROUP * j + SPAN, 0:loads])
+            both = mm(gram[j], a_high)
+            parts.append(both[:SPAN] + both[SPAN:] + mm(gram[j, 0:SPAN], a_low))
         rows = []
         for j in range(clusters):
             line = parts[j][GROUP : 2 * GROUP]
@@ -361,9 +313,9 @@
                 both = both[:rows] + both[rows:]
             out[:, cols] = (weight * weight) * both
 
-    def permute(src, order, dst):
+    def permute(src, order, dst, span=range(chunks)):
         rows = src.shape[0]
-        for t in range(chunks):
+        for t in span:
             cols = slice(t * LANES, (t + 1) * LANES)
             line = jnp.broadcast_to(order[0:1, cols], (rows, LANES))
             lane, chunk = line & (LANES - 1), line >> 7
@@ -375,6 +327,19 @@
                 found = jnp.where(chunk == u, seen, found)
             dst[:, cols] = found
 
+    def apply(src, dst, parts):
+        total = None
+        step = 2 * LANES
+        for t in range(slots // step):
+            cols = slice(t * step, (t + 1) * step)
+            permute(src, inverse, dst, range(2 * t, 2 * t + 2))
+            pieces = jnp.concatenate(split(dst[:, cols])[:parts], axis=0)
+            part = mm(pieces, oper[cols, :])
+            total = part if total is None else total + part
+        if parts == 2:
+            total = total[:loads] + total[loads:]
+        return softness * total
+
     softness = 1.0 / jnp.broadcast_to(stiff_ref[...], (loads, LANES))
     softness = jnp.concatenate([softness] * chunks, axis=1)
 
@@ -383,6 +348,61 @@
 
     start_faces(basis_args)
     start_faces(halo_args[0])
+
+    zero_tile = jnp.zeros((WIDE, LANES), F32)
+    for k in range(SUMS):
+        ybuf[k, y] = zero_tile
+        for core_id in range(CORES):
+            zbuf[k, 0, core_id] = zero_tile
+            zbuf[k, nz + 1, core_id] = zero_tile
+    amount[...] = jnp.zeros_like(amount)
+
+    @pl.when(jnp.logical_not(has_prev))
+    def _():
+        nbr_basis[0] = jnp.zeros((GROUP, face), F32)
+        halo_span[0] = jnp.zeros((SPAN, face), F32)
+        for k in range(HALOS):
+            halo[k, 0] = jnp.zeros((loads, face), F32)
+
+    @pl.when(jnp.logical_not(has_next))
+    def _():
+        nbr_basis[1] = jnp.zeros((GROUP, face), F32)
+        halo_span[1] = jnp.zeros((SPAN, face), F32)
+        for k in range(HALOS):
+            halo[k, 1] = jnp.zeros((loads, face), F32)
+
+    coarse_size = coarse_ref.shape[0]
+    total_rows = clusters * GROUP
+
+    def placed(row, entry):
+        return jnp.where((modes * (row >> 3) + (row & 7) == entry) & ((row & 7) < modes), 1.0, 0.0)
+
+    shape = (total_rows, coarse_size)
+    down = placed(lax.broadcasted_iota(jnp.int32, shape, 0), lax.broadcasted_iota(jnp.int32, shape, 1))
+    shape = (coarse_size, total_rows)
+    across = placed(
+        lax.broadcasted_iota(jnp.int32, shape, 1), lax.broadcasted_iota(jnp.int32, shape, 0)
+    )
+    c_high, c_low = split(exact(exact(down, coarse_ref[...]), across))
+    coarse[0:total_rows] = c_high
+    coarse[total_rows:] = c_low
+
+    def invert(t, carry):
+        where = t * LANES + lax.broadcasted_iota(jnp.int32, (LANES, LANES), 0)
+        found = jnp.zeros((LANES, LANES), F32)
+        for u in range(chunks):
+            here = (u * LANES + lax.broadcasted_iota(jnp.int32, (LANES, LANES), 1)).astype(F32)
+            line = jnp.broadcast_to(index_ref[:, u * LANES : (u + 1) * LANES], (LANES, LANES))
+            found = jnp.where(line == where, here, found)
+        line = jnp.sum(found.T, axis=0, keepdims=True).astype(jnp.int32)
+        inverse[:, pl.ds(pl.multiple_of(t * LANES, LANES), LANES)] = jnp.broadcast_to(
+            line, (GROUP, LANES)
+        )
+        return carry
+
+    lax.fori_loop(0, chunks, invert, 0)
+    blocks_copy.wait()
+
     wait_faces(basis_args)
     low, high = nbr_basis[0], nbr_basis[1]
     at_first, at_last = first_m.astype(F32), last_m.astype(F32)
@@ -435,21 +455,23 @@
         order_h[SPAN : 2 * SPAN] = t_high
         order_l[SPAN : 2 * SPAN] = t_low
 
-    def start_first():
-        start_faces(span_args)
-        start_faces(halo_args[1])
-
-    reduce(0, WIDE, nothing, start_first, assemble_span)
+    reduce(
+        0, WIDE, lambda: start_faces(span_args), lambda: start_faces(halo_args[1]), assemble_span
+    )
     parts = gathered(0)
     for j in range(clusters):
-        gram[j] = jnp.concatenate(
+        square = jnp.concatenate(
             [
                 parts[j + 2, 0:GROUP, loads : loads + SPAN],
                 parts[j + 2, 0:GROUP, loads + SPAN : LANES],
                 parts[j + 2, 2 * GROUP : WIDE, loads : loads + SPAN],
+                jnp.zeros((GROUP, SPAN), F32),
             ],
             axis=0,
         )
+        g_high, g_low = split(square)
+        gram[j, 0:SPAN] = g_high
+        gram[j, SPAN : 2 * SPAN] = g_low
     totals = parts[2 : 2 + clusters, GROUP : 2 * GROUP, LANES - loads : LANES]
     amount_r = solve(totals.reshape(total_rows, loads))
     reduced = fold(parts)[:, 0:loads] - gram_amount()
@@ -460,9 +482,8 @@
     )
     proj[...] = resid[...] - expand(amount_r, SPAN)
 
-    permute(search0, inverse, turned0)
     oper_copy.wait()
-    image0[...] = softness * mm(turned0[...].astype(BF16), oper[...])
+    image0[...] = apply(search0, turned0, 1)
     terms = restrict(order_h[...], order_l[...], image0[...])
     ybuf[1, y] = jnp.concatenate([terms[0:WIDE], terms[SPAN : SPAN + WIDE]], axis=1)
     ybuf[1, y, 2 * GROUP - 2 : 2 * GROUP - 1, 0:loads] = row_sum(weighted(proj[...]) * search0[...])
@@ -492,10 +513,7 @@
     wait_faces(halo_args[3])
     search1[...] = assembled(3, sent[2]) - spread_y
 
-    permute(search1, inverse, turned1)
-    t_high, t_low = split(turned1[...])
-    both = mm(jnp.concatenate([t_high, t_low], axis=0), oper[...])
-    image1[...] = softness * (both[:loads] + both[loads:])
+    image1[...] = apply(search1, turned1, 2)
     ybuf[2, y, 0:1, 0:loads] = row_sum(weighted(proj[...]) * search1[...])
     ybuf[2, y, 1:2, 0:loads] = row_sum(turned1[...] * image1[...])
     ybuf[2, y, 2:3, 0:loads] = row_sum(turned1[...] * image0[...])
@@ -554,7 +572,7 @@
     load = dual_load.reshape(loads, 2, face // LANES, LANES).transpose(0, 2, 1, 3)
     outs = pl.pallas_call(
         kernel,
-        out_shape=[jax.ShapeDtypeStruct((rows, LANES), F32)] * 2,
+        out_shape=[pltpu.VMEM((rows, LANES), F32)] * 2,
         in_specs=[vmem] * 4 + [in_place] * 3,
         out_specs=[vmem] * 2,
         scratch_shapes=[
@@ -570,9 +588,9 @@
             spans,
             spans,
             span,
-            pltpu.VMEM((clusters * GROUP, clusters * GROUP), F32),
+            pltpu.VMEM((2 * clusters * GROUP, clusters * GROUP), BF16),
             pltpu.VMEM(((clusters + 3) * GROUP, LANES), F32),
-            pltpu.VMEM((clusters, WIDE, SPAN), F32),
+            pltpu.VMEM((clusters, 2 * SPAN, SPAN), BF16),
             pltpu.VMEM((GROUP, slots), jnp.int32),
             pltpu.VMEM((HALOS, 2, loads, face), F32),
             pltpu.VMEM((2, SPAN, face), F32),
@@ -594,7 +612,7 @@
         ]
         + [dma((SUMS,))] * 8,
         compiler_params=pltpu.CompilerParams(
-            collective_id=0, has_side_effects=True, vmem_limit_bytes=56 * 2**20
+            collective_id=0, has_side_effects=True, vmem_limit_bytes=62 * 2**20
         ),
         name="pcpg",
     )(

time: 117 us -> 109 us (0.932)
  Pallas kernels: 111 us -> 105 us
  local copies, waits for them, and re-layouts: 3.74 us -> 1.59 us
    pallas_call x1, Pallas kernels: 111 us -> 105 us  [per_device(): pl.pallas_call(kernel, out_shape=[pltpu.VMEM((rows, LANES), F32)] * 2, in...]
    unnamed x2, local copies, waits for them, and re-layouts: 3.74 us -> 1.59 us
where the time goes in v3:
time: 109 us; the launch traced here: 108 us
  Pallas kernels  105 us (96%)
  local copies, waits for them, and re-layouts  1.59 us (1%)
  between operations  1.29 us (1%)
    pallas_call x1, Pallas kernels, per_device(): pl.pallas_call(kernel, out_shape=[pltpu.VMEM((rows, LANES), F32)] * 2, in...  105 us

profile of v3, /device:TPU:1, one launch (start us, length us, event | category | flops | bytes accessed | tf_op | source)
XLA Modules:
  0.0 108.0 jit_solution(17032535813855870298)
XLA Ops:
  1.3 105.2 %pcpg.1 = (f32[1024,128]{1,0:T(8,128)S(1)}, f32[1024,128]{1,0:T(8,128)S(1)}) custom-call(f32[6,1,2048]{2,1,0:T(1,128)} %bitcast.22, f32[144,144]{1,0:T(8,128)} %coarse_ref.1, s32[1,2048]{1,0:T(1,128)} %bitcast.23, f32[1,1]{1,0:T(1,128)S(6)} %copy.16.stiff_ref, f32[1024,128]{1,0:T(8,128)} %bitcast.20, bf16[16,128,128]{2,1,0:T(8,128)(2,1)} %bitcast.21, ...), custom_call_target="tpu_custom_call" | custom-call | tf_op jit(solution)/shard_map/pcpg/pallas_call | solution.py:573
  106.4 0.8 copy.14
  107.2 0.8 copy.15

commit v4 on v3

--- a/solution.py
+++ b/solution.py
@@ -36,15 +36,18 @@
 
 
 def kernel(
-    basis_ref,
-    coarse_ref,
-    index_ref,
     stiff_ref,
+    basis_hbm,
+    coarse_hbm,
+    index_hbm,
     load_hbm,
     blocks_hbm,
     oper_hbm,
     mult_out,
     resid_out,
+    basis_ref,
+    coarse_ref,
+    index_ref,
     raw,
     blocks,
     oper,
@@ -113,9 +116,13 @@
     first_m, last_m = m == 0, m == members - 1
     prev = (jnp.where(first_m, c - 1, c), jnp.where(first_m, members - 1, m - 1))
     nxt = (jnp.where(last_m, c + 1, c), jnp.where(last_m, 0, m + 1))
-    y_peers = [(c, x * ny + lax.rem(y + i, ny)) for i in range(1, ny)]
-    x_peers = [(c, lax.rem(x + i, nx) * ny + y) for i in range(1, nx)]
-    z_peers = [(lax.rem(z + i, nz) * CORES + core, m) for i in range(1, nz)]
+
+    def far_first(count):
+        return sorted(range(1, count), key=lambda i: -min(i, count - i))
+
+    y_peers = [(c, x * ny + lax.rem(y + i, ny)) for i in far_first(ny)]
+    x_peers = [(c, lax.rem(x + i, nx) * ny + y) for i in far_first(nx)]
+    z_peers = [(lax.rem(z + i, nz) * CORES + core, m) for i in far_first(nz)]
     partner = (z * CORES + 1 - core, m)
 
     def copy(src, dst, ss, rs, device):
@@ -142,11 +149,14 @@
     raw_copy = pltpu.make_async_copy(load_hbm, raw, local_sem.at[0])
     blocks_copy = pltpu.make_async_copy(blocks_hbm, blocks, local_sem.at[1])
     oper_copy = pltpu.make_async_copy(oper_hbm, oper, local_sem.at[2])
-    raw_copy.start()
-    blocks_copy.start()
-    oper_copy.start()
+    basis_copy = pltpu.make_async_copy(basis_hbm, basis_ref, local_sem.at[3])
+    coarse_copy = pltpu.make_async_copy(coarse_hbm, coarse_ref, local_sem.at[4])
+    index_copy = pltpu.make_async_copy(index_hbm, index_ref, local_sem.at[5])
+    for each in (basis_copy, raw_copy, coarse_copy, index_copy, blocks_copy, oper_copy):
+        each.start()
 
     own_basis[...] = jnp.zeros_like(own_basis)
+    basis_copy.wait()
     for k in range(modes):
         own_basis[k : k + 1, :] = basis_ref[k]
     raw_copy.wait()
@@ -371,6 +381,8 @@
         for k in range(HALOS):
             halo[k, 1] = jnp.zeros((loads, face), F32)
 
+    coarse_copy.wait()
+    index_copy.wait()
     coarse_size = coarse_ref.shape[0]
     total_rows = clusters * GROUP
 
@@ -573,9 +585,12 @@
     outs = pl.pallas_call(
         kernel,
         out_shape=[pltpu.VMEM((rows, LANES), F32)] * 2,
-        in_specs=[vmem] * 4 + [in_place] * 3,
+        in_specs=[vmem] + [in_place] * 6,
         out_specs=[vmem] * 2,
         scratch_shapes=[
+            pltpu.VMEM((modes, 1, slots), F32),
+            pltpu.VMEM(coarse_inverse.shape, F32),
+            pltpu.VMEM((1, slots), jnp.int32),
             pltpu.VMEM((rows, LANES), F32),
             pltpu.VMEM(blocks_shape, BF16),
             pltpu.VMEM((slots, slots), BF16),
@@ -602,7 +617,7 @@
             pltpu.VMEM((SUMS, ny, WIDE, LANES), F32),
             pltpu.VMEM((SUMS, nx, WIDE, LANES), F32),
             pltpu.VMEM((SUMS, nz + 2, CORES, WIDE, LANES), F32),
-            dma((3,)),
+            dma((6,)),
             dma((2,)),
             dma((2,)),
             dma((2,)),
@@ -616,10 +631,10 @@
         ),
         name="pcpg",
     )(
+        stiffness,
         coarse_basis.reshape(modes, 1, slots),
         coarse_inverse,
         index_map.reshape(1, slots),
-        stiffness,
         load.reshape(rows, LANES),
         dirichlet_blocks.reshape(blocks_shape),
         dual_operator,

time: 109 us -> 110 us (level)
  Pallas kernels: 105 us -> 107 us
    pallas_call x1, Pallas kernels: 105 us -> 107 us  [per_device(): pl.pallas_call(kernel, out_shape=[pltpu.VMEM((rows, LANES), F32)] * 2, in...]
where the time goes in v4:
time: 110 us
  Pallas kernels  107 us (97%)
  local copies, waits for them, and re-layouts  1.59 us (1%)
  between operations  1.29 us (1%)
    pallas_call x1, Pallas kernels, per_device(): pl.pallas_call(kernel, out_shape=[pltpu.VMEM((rows, LANES), F32)] * 2, in...  107 us

profile of v4, /device:TPU:1, one launch (start us, length us, event | category | flops | bytes accessed | tf_op | source)
XLA Modules:
  0.0 110.1 jit_solution(15589155551842201259)
XLA Ops:
  1.3 107.2 %pcpg.1 = (f32[1024,128]{1,0:T(8,128)S(1)}, f32[1024,128]{1,0:T(8,128)S(1)}) custom-call(f32[1,1]{1,0:T(1,128)S(6)} %copy.16.stiff_ref, f32[6,1,2048]{2,1,0:T(1,128)} %bitcast.22, f32[144,144]{1,0:T(8,128)} %coarse_hbm.1, s32[1,2048]{1,0:T(1,128)} %bitcast.23, f32[1024,128]{1,0:T(8,128)} %bitcast.20, bf16[16,128,128]{2,1,0:T(8,128)(2,1)} %bitcast.21, ...), custom_call_target="tpu_custom_call" | custom-call | tf_op jit(solution)/shard_map/pcpg/pallas_call | solution.py:585
  108.5 0.8 copy.14
  109.3 0.8 copy.15
